TPU v7x, 32 devices: a whole 2x2x4 slice. The times are simulated.
32 devices in a mesh: expert: 4 (over y, x), cuts: 8 (over z, core).
Axes of the slice: x: 2, y: 2, z: 4, core: 2. Of those that a mesh axis runs over, the one named last changes fastest.
Arguments:
- token_rows: bfloat16 [4, 1152, 4096], P('expert', 'cuts'), may hold values from -6 to 6
- cotangent: bfloat16 [4, 1152, 4096], P('expert', 'cuts'), may hold values from -6 to 6
- counts: int32 [4], replicated, may hold values from 384 to 1152, as said below
- gate_master: float32 [4, 1152, 4096], P(None, 'cuts', 'expert'), may hold values from -0.09375 to 0.09375
- up_master: float32 [4, 1152, 4096], P(None, 'cuts', 'expert'), may hold values from -0.09375 to 0.09375
- down_master: float32 [4, 1152, 4096], P(None, 'cuts', 'expert'), may hold values from -0.1875 to 0.1875
- gate_first: float32 [4, 1152, 4096], P(None, 'cuts', 'expert'), may hold values from -60 to 60
- up_first: float32 [4, 1152, 4096], P(None, 'cuts', 'expert'), may hold values from -60 to 60
- down_first: float32 [4, 1152, 4096], P(None, 'cuts', 'expert'), may hold values from -60 to 60
- gate_second: float32 [4, 1152, 4096], P(None, 'cuts', 'expert'), may hold values from 100 to 1000
- up_second: float32 [4, 1152, 4096], P(None, 'cuts', 'expert'), may hold values from 100 to 1000
- down_second: float32 [4, 1152, 4096], P(None, 'cuts', 'expert'), may hold values from 100 to 1000
Outputs:
- out_rows: bfloat16 [4, 1152, 4096], P('expert', 'cuts')
- input_grads: bfloat16 [4, 1152, 4096], P('expert', 'cuts')
- new_gate_master: float32 [4, 1152, 4096], P(None, 'cuts', 'expert')
- new_up_master: float32 [4, 1152, 4096], P(None, 'cuts', 'expert')
- new_down_master: float32 [4, 1152, 4096], P(None, 'cuts', 'expert')
- new_gate_first: float32 [4, 1152, 4096], P(None, 'cuts', 'expert')
- new_up_first: float32 [4, 1152, 4096], P(None, 'cuts', 'expert')
- new_down_first: float32 [4, 1152, 4096], P(None, 'cuts', 'expert')
- new_gate_second: float32 [4, 1152, 4096], P(None, 'cuts', 'expert')
- new_up_second: float32 [4, 1152, 4096], P(None, 'cuts', 'expert')
- new_down_second: float32 [4, 1152, 4096], P(None, 'cuts', 'expert')
Inputs may be any that keep to these rules, and one draw needn't show every extreme that they name: `counts`: some expert has exactly 1152 live rows in every draw.
All inputs are finite; a program needn't handle non-finite values.
Results may differ from a plain program's by a relative error of at most 0.015.
Values may be sent and summed in bfloat16 or wider, within the bound.
No kernel may reach another device: no remote copies, remote signals or barrier semaphores. Data moves between devices by JAX's collectives and lax.ppermute only.
A program may use at most 192 MiB of HBM per device.

v0:
```python
import functools
import jax
import jax.numpy as jnp
from jax import lax
from jax.experimental import pallas as pl
from jax.experimental.pallas import tpu as pltpu
from jax.sharding import PartitionSpec as P

beta_first = 0.9
beta_second = 0.95
learn_rate = 0.01
decay_rate = 0.1
epsilon = 1e-08


def adam_kernel(count, order_ref, *refs):
    pieces, (master, first, second) = refs[:count], refs[count:count + 3]
    new_master, new_first, new_second = refs[count + 3:]
    turn = pl.program_id(0)
    grads = pieces[0][...].astype(jnp.float32)
    for other in range(1, count):
        grads = jnp.where(turn == other, pieces[other][...].astype(jnp.float32), grads)
    first_new = beta_first * first[0] + (1.0 - beta_first) * grads
    second_new = beta_second * second[0] + (1.0 - beta_second) * grads * grads
    new_master[0] = master[0] - learn_rate * (
        first_new / (jnp.sqrt(second_new) + epsilon) + decay_rate * master[0]
    )
    new_first[0] = first_new
    new_second[0] = second_new


def adam_update(order, pieces, master, first, second):
    count, units, cols = master.shape
    state = pl.BlockSpec((1, units, cols), lambda t, order: (order[t], 0, 0))
    piece = pl.BlockSpec((units, cols), lambda t, order: (0, 0))
    return pl.pallas_call(
        functools.partial(adam_kernel, count),
        grid_spec=pltpu.PrefetchScalarGridSpec(
            num_scalar_prefetch=1,
            grid=(count,),
            in_specs=[piece] * count + [state] * 3,
            out_specs=[state] * 3,
        ),
        out_shape=[jax.ShapeDtypeStruct(master.shape, jnp.float32)] * 3,
        compiler_params=pltpu.CompilerParams(vmem_limit_bytes=20 << 20),
        cost_estimate=pl.CostEstimate(
            flops=16 * master.size, transcendentals=master.size, bytes_accessed=26 * master.size
        ),
        name="adam",
    )(order, *pieces, master, first, second)


def join_kernel(count, order_ref, *refs):
    turn = pl.program_id(0)
    value = refs[0][...]
    for other in range(1, count):
        value = jnp.where(turn == other, refs[other][...], value)
    refs[count][...] = value


def join(order, pieces):
    count, (units, cols) = len(pieces), pieces[0].shape
    return pl.pallas_call(
        functools.partial(join_kernel, count),
        grid_spec=pltpu.PrefetchScalarGridSpec(
            num_scalar_prefetch=1,
            grid=(count,),
            in_specs=[pl.BlockSpec((units, cols), lambda t, order: (0, 0))] * count,
            out_specs=pl.BlockSpec((units, cols), lambda t, order: (0, order[t])),
        ),
        out_shape=jax.ShapeDtypeStruct((units, count * cols), pieces[0].dtype),
        compiler_params=pltpu.CompilerParams(vmem_limit_bytes=8 << 20),
        cost_estimate=pl.CostEstimate(
            flops=0, transcendentals=0, bytes_accessed=4 * count * units * cols
        ),
        name="join",
    )(order, *pieces)


def dot_t(a, b):
    return lax.dot_general(a, b, (((1,), (1,)), ((), ())), preferred_element_type=jnp.float32)


def dot_n(a, b):
    return lax.dot_general(a, b, (((1,), (0,)), ((), ())), preferred_element_type=jnp.float32)


def dot_0(a, b):
    return lax.dot_general(a, b, (((0,), (0,)), ((), ())), preferred_element_type=jnp.float32)


def device_at(core, place, chips):
    chip = place if core == 0 else chips - 1 - place
    return 2 * chip + core


def hop(value, way, chips):
    pairs = []
    for core in range(2):
        for place in range(chips):
            last = place == chips - 1
            here = device_at(core, place, chips)
            there = device_at(1 - core if last else core, 0 if last else place + 1, chips)
            pairs.append((here, there) if way == 1 else (there, here))
    return lax.ppermute(value, "cuts", pairs)


def swap_cores(value, chips):
    pairs = [(2 * s + c, 2 * s + 1 - c) for s in range(chips) for c in range(2)]
    return lax.ppermute(value, "cuts", pairs)


def partner(index, turn, count):
    if count & (count - 1) == 0:
        return index ^ turn
    return (turn - index) % count


def plan_line(n):
    have = [{("T", p): None, ("C", p): None} for p in range(n)]
    made = [{} for _ in range(n)]
    came = {1: [{} for _ in range(n)], -1: [{} for _ in range(n)]}
    sends, works = [], []
    need = {}
    for d in (1, -1):
        for p in range(n):
            if 0 <= p + d < n:
                before = [b for b in range(n) if (b - p) * d <= 0]
                after = [b for b in range(n) if (b - p) * d > 0]
                need[d, p] = [("T", b) for b in sorted(before, key=lambda b: abs(b - p))]
                need[d, p] += [("C", b) for b in sorted(before, key=lambda b: -abs(b - p))]
                need[d, p] += [("O", b) for b in sorted(after, key=lambda b: -abs(b - p))]
                need[d, p] += [("I", b) for b in sorted(after, key=lambda b: -abs(b - p))]
    todo = [{k: [b for b in range(n) if b != p] for k in "TC"} for p in range(n)]

    def rank(p, kind, b):
        long_side = (b > p) == (2 * p < n - 1)
        return (not long_side, abs(b - p) if kind == "T" else -abs(b - p))

    step = 0
    while any(need.values()) or any(t[k] for t in todo for k in "TC"):
        sent, work = {}, {}
        for (d, p), left in need.items():
            for m in left:
                kind, b = m
                if kind in "TC":
                    ready = m in have[p]
                    terms = (have[p].get(m, ("own", kind)) or ("own", kind), None)
                else:
                    first = not 0 <= p - d < n
                    ready = b in made[p].get(kind, {}) and (first or m in came[d][p])
                    if ready:
                        terms = (made[p][kind][b], None if first else came[d][p][m])
                if ready:
                    sent[d, p] = (m, terms)
                    left.remove(m)
                    break
        for p in range(n):
            for kind in "TC":
                if kind == "C" and step < n:
                    continue
                can = [b for b in todo[p][kind] if (kind, b) in have[p]]
                if can:
                    b = min(can, key=lambda b: rank(p, kind, b))
                    todo[p][kind].remove(b)
                    work[kind, p] = (b, have[p][kind, b])
        for (d, p), (m, _) in sent.items():
            name = ("got", d, step)
            if m[0] in "TC":
                have[p + d][m] = name
            else:
                came[d][p + d][m] = name
        for (kind, p), (b, _) in work.items():
            made[p].setdefault({"T": "O", "C": "I"}[kind], {})[b] = ("made", kind, step)
        sends.append(sent)
        works.append(work)
        step += 1
    return sends, works, came


def pick(place, options, like):
    values = []
    for p, value in options.items():
        for entry in values:
            if entry[0] is value:
                entry[1].append(p)
                break
        else:
            values.append((value, [p]))
    if not values:
        return like
    values.sort(key=lambda entry: len(entry[1]))
    result = values[-1][0]
    for value, places in values[:-1]:
        here = place == places[0]
        for p in places[1:]:
            here = here | (place == p)
        result = jnp.where(here, value, result)
    return result


def make_shards(chips, experts):
    sends, works, came = plan_line(chips)

    def shards(
        token_rows, cotangent, counts,
        gate_master, up_master, down_master,
        gate_first, up_first, down_first,
        gate_second, up_second, down_second,
    ):
        local_rows = token_rows.shape[1]
        cut = lax.axis_index("cuts")
        core = cut % 2
        place = jnp.where(core == 0, cut // 2, chips - 1 - cut // 2)
        live = counts[lax.axis_index("expert")]
        own_row = jnp.arange(local_rows, dtype=jnp.int32) + cut * local_rows
        keep = (own_row < live)[:, None]
        own_t = token_rows[0]
        own_c = jnp.where(keep, cotangent[0], jnp.zeros_like(cotangent[0]))
        own_c = lax.optimization_barrier(own_c)

        me = lax.axis_index("expert")
        cols = gate_master.shape[2]

        order = jnp.stack([partner(me, turn, experts) for turn in range(experts)]).astype(jnp.int32)

        def trade(pieces):
            return [pieces[0]] + [
                lax.ppermute(pieces[turn], "expert", [(e, partner(e, turn, experts)) for e in range(experts)])
                for turn in range(1, experts)
            ]

        def fetch(master):
            pieces = [
                lax.dynamic_index_in_dim(master, order[turn], 0, keepdims=False).astype(jnp.bfloat16)
                for turn in range(experts)
            ]
            pieces = trade(pieces)
            whole = join(order, pieces)
            both = jnp.concatenate([whole, swap_cores(whole, chips)], axis=0)
            return lax.optimization_barrier(both)

        gate_w, up_w, down_w = fetch(gate_master), fetch(up_master), fetch(down_master)

        def forward(block):
            gate_pre = dot_t(block, gate_w)
            up_pre = dot_t(block, up_w)
            hidden = (gate_pre * jax.nn.sigmoid(gate_pre) * up_pre).astype(jnp.bfloat16)
            return gate_pre, up_pre, hidden, dot_n(hidden, down_w).astype(jnp.bfloat16)

        def backward(block, gate_pre, up_pre):
            grad_hidden = dot_t(block, down_w)
            sig = jax.nn.sigmoid(gate_pre)
            d_gate = (grad_hidden * up_pre * sig * (1.0 + gate_pre * (1.0 - sig))).astype(jnp.bfloat16)
            d_up = (grad_hidden * (gate_pre * sig)).astype(jnp.bfloat16)
            return d_gate, d_up, (dot_n(d_gate, gate_w) + dot_n(d_up, up_w)).astype(jnp.bfloat16)

        arrays = {("own", "T"): own_t, ("own", "C"): own_c}
        t_work, c_work, t_got, c_got = [], [], {}, {}
        own_places = {p: p for p in range(chips)}
        t_steps = [i for i, work in enumerate(works) if any(k == "T" for k, _ in work)]
        c_steps = [i for i, work in enumerate(works) if any(k == "C" for k, _ in work)]
        own_with = {"T": t_steps[len(t_steps) // 2], "C": c_steps[len(c_steps) // 2]}

        def of_block(wanted, steps, got, item):
            where_made = {}
            for p, b in wanted.items():
                for name, blocks in steps:
                    if blocks.get(p) == b:
                        where_made[p] = got[name][item]
            result = pick(place, where_made, None)
            idle = [p for p in range(chips) if p not in wanted]
            for p in idle:
                result = jnp.where(place == p, jnp.zeros_like(result), result)
            return result

        last_sent = own_t
        for step, (sent, work) in enumerate(zip(sends, works)):
            for d in (1, -1):
                before = ("got", d, step - 1)
                if before in arrays:
                    arrays[before] = lax.optimization_barrier((arrays[before], last_sent))[0]
                firsts = {p: arrays[terms[0]] for (e, p), (_, terms) in sent.items() if e == d}
                if not firsts:
                    continue
                value = pick(place, firsts, None)
                seconds = {p: arrays[terms[1]] for (e, p), (_, terms) in sent.items() if e == d and terms[1]}
                if seconds:
                    more = pick(place, seconds, None)
                    here = jnp.zeros((), jnp.bool_)
                    for p in seconds:
                        here = here | (place == p)
                    more = jnp.where(here, more, jnp.zeros_like(more))
                    value = value + more
                last_sent = value
                came_in = hop(value, d, chips)
                arrays["got", d, step] = came_in
            for kind in "TC":
                blocks = {p: b for (k, p), (b, _) in work.items() if k == kind}
                if not blocks:
                    continue
                block = pick(place, {p: arrays[name] for (k, p), (_, name) in work.items() if k == kind}, None)
                with_own = own_with[kind] == step
                batch = [(step, blocks, block)]
                if with_own:
                    batch.append(("own", own_places, arrays["own", kind]))
                joined = jnp.concatenate([entry[2] for entry in batch], axis=0)
                if kind == "T":
                    results = forward(joined)
                else:
                    pres = [
                        jnp.concatenate([of_block(entry[1], t_work, t_got, item) for entry in batch], axis=0)
                        for item in (1, 2)
                    ]
                    results = backward(joined, *pres)
                results = [jnp.split(value, len(batch), axis=0) for value in results]
                for i, (name, its_blocks, its_block) in enumerate(batch):
                    mine = [value[i] for value in results]
                    mine[-1] = lax.optimization_barrier(mine[-1])
                    (t_work if kind == "T" else c_work).append((name, its_blocks))
                    (t_got if kind == "T" else c_got)[name] = (its_block, *mine)
                    arrays["made", kind, name] = mine[-1]

        def total(own, kind):
            result = lax.optimization_barrier((own, last_sent))[0].astype(jnp.float32)
            ends = {p: [came[d][p][kind, p] for d in (1, -1) if (kind, p) in came[d][p]] for p in range(chips)}
            for turn in range(2):
                terms = {p: arrays[names[turn]] for p, names in ends.items() if len(names) > turn}
                if not terms:
                    continue
                uses = {}
                for p, value in terms.items():
                    uses.setdefault(id(value), (value, []))[1].append(p)
                late = {}
                for value, places in uses.values():
                    value = lax.optimization_barrier((value, last_sent))[0]
                    late.update({p: value for p in places})
                more = pick(place, late, None)
                if len(late) < chips:
                    here = jnp.zeros((), jnp.bool_)
                    for p in late:
                        here = here | (place == p)
                    more = jnp.where(here, more, jnp.zeros_like(more))
                result = result + more.astype(jnp.float32)
            return result

        out_rows = jnp.where(keep, total(arrays["made", "T", "own"], "O"), 0.0).astype(jnp.bfloat16)[None]
        input_grads = total(arrays["made", "C", "own"], "I").astype(jnp.bfloat16)[None]

        tokens = jnp.concatenate([t_got[name][0] for name, _ in t_work], axis=0)
        upstream = jnp.concatenate([c_got[name][0] for name, _ in c_work], axis=0)
        hidden = jnp.concatenate([of_block(blocks, t_work, t_got, 3) for _, blocks in c_work], axis=0)
        d_gate = jnp.concatenate([of_block(blocks, c_work, c_got, 1) for _, blocks in t_work], axis=0)
        d_up = jnp.concatenate([of_block(blocks, c_work, c_got, 2) for _, blocks in t_work], axis=0)

        def collect(left, right):
            grad = dot_0(left, right).astype(jnp.bfloat16)
            units = grad.shape[0] // 2
            summed = grad[:units].astype(jnp.float32) + swap_cores(grad[units:], chips).astype(jnp.float32)
            summed = summed.astype(jnp.bfloat16)
            pieces = [
                lax.dynamic_slice_in_dim(summed, order[turn] * cols, cols, axis=1) for turn in range(experts)
            ]
            return trade(pieces)

        down_grads = collect(hidden, upstream)
        gate_grads = collect(d_gate, tokens)
        up_grads = collect(d_up, tokens)
        down_new = adam_update(order, down_grads, down_master, down_first, down_second)
        gate_new = adam_update(order, gate_grads, gate_master, gate_first, gate_second)
        up_new = adam_update(order, up_grads, up_master, up_first, up_second)
        return (
            out_rows, input_grads,
            gate_new[0], up_new[0], down_new[0],
            gate_new[1], up_new[1], down_new[1],
            gate_new[2], up_new[2], down_new[2],
        )

    return shards


def solution(mesh):
    rows, states = P("expert", "cuts", None), P(None, "cuts", "expert")
    chips = mesh.shape["cuts"] // 2
    shards = make_shards(chips, mesh.shape["expert"])

    return jax.shard_map(
        shards,
        mesh=mesh,
        in_specs=(rows, rows, P()) + (states,) * 9,
        out_specs=(rows, rows) + (states,) * 9,
        check_vma=False,
    )
```

profile of v0, /device:TPU:0, one launch (start us, length us, event | category | flops | bytes accessed | tf_op | source)
XLA Modules:
  0.0 282.0 jit_solution(13770845003942866481)
XLA Ops:
  0.7 2.7 fusion.49
  3.4 3.9 %collective-permute-start.9 = (bf16[144,1024]{1,0:T(8,128)(2,1)S(1)}, bf16[144,1024]{1,0:T(8,128)(2,1)S(1)}, u32[]{:S(2)}, u32[]{:S(2)}) collective-permute-start(bf16[144,1024]{1,0:T(8,128)(2,1)S(1)} %get-tuple-element.95), channel_id=1, source_target_pairs={{0,24},{8,16},{16,8},{24,0},{1,25},{9,17},{17,9},{25,1},{2,26},{10... | collective-permute-start | bytes 884744 | tf_op jit(solution)/shard_map/ppermute | solution.py:229
  8.9 2.9 %collective-permute-start.13 = (bf16[144,1024]{1,0:T(8,128)(2,1)}, bf16[144,1024]{1,0:T(8,128)(2,1)}, u32[]{:S(2)}, u32[]{:S(2)}) collective-permute-start(bf16[144,1024]{1,0:T(8,128)(2,1)} %get-tuple-element.87), channel_id=1, source_target_pairs={{0,24},{8,16},{16,8},{24,0},{1,25},{9,17},{17,9},{25,1},{2,26},{10... | collective-permute-start | bytes 884744 | tf_op jit(solution)/shard_map/ppermute | solution.py:229
  12.3 2.9 %collective-permute-done.9.refs_3_ = bf16[144,1024]{1,0:T(8,128)(2,1)S(1)} collective-permute-done((bf16[144,1024]{1,0:T(8,128)(2,1)S(1)}, bf16[144,1024]{1,0:T(8,128)(2,1)S(1)}, u32[]{:S(2)}, u32[]{:S(2)}) %collective-permute-start.9) | collective-permute-done | bytes 294944 | tf_op jit(solution)/shard_map/ppermute | solution.py:229
  18.8 2.9 %collective-permute-done.8.refs_2_ = bf16[144,1024]{1,0:T(8,128)(2,1)} collective-permute-done((bf16[144,1024]{1,0:T(8,128)(2,1)}, bf16[144,1024]{1,0:T(8,128)(2,1)}, u32[]{:S(2)}, u32[]{:S(2)}) %collective-permute-start.8) | collective-permute-done | bytes 294944 | tf_op jit(solution)/shard_map/ppermute | solution.py:229
  21.7 2.1 collective-permute-start.1
  24.4 3.6 %collective-permute-done.13.refs_3_ = bf16[144,1024]{1,0:T(8,128)(2,1)} collective-permute-done((bf16[144,1024]{1,0:T(8,128)(2,1)}, bf16[144,1024]{1,0:T(8,128)(2,1)}, u32[]{:S(2)}, u32[]{:S(2)}) %collective-permute-start.13) | collective-permute-done | bytes 294944 | tf_op jit(solution)/shard_map/ppermute | solution.py:229
  28.0 2.9 %collective-permute-start.5 = (bf16[144,1024]{1,0:T(8,128)(2,1)}, bf16[144,1024]{1,0:T(8,128)(2,1)}, u32[]{:S(2)}, u32[]{:S(2)}) collective-permute-start(bf16[144,1024]{1,0:T(8,128)(2,1)} %get-tuple-element.91), channel_id=1, source_target_pairs={{0,24},{8,16},{16,8},{24,0},{1,25},{9,17},{17,9},{25,1},{2,26},{10... | collective-permute-start | bytes 884744 | tf_op jit(solution)/shard_map/ppermute | solution.py:229
  30.9 3.3 %collective-permute-done.12.refs_2_ = bf16[144,1024]{1,0:T(8,128)(2,1)} collective-permute-done((bf16[144,1024]{1,0:T(8,128)(2,1)}, bf16[144,1024]{1,0:T(8,128)(2,1)}, u32[]{:S(2)}, u32[]{:S(2)}) %collective-permute-start.12) | collective-permute-done | bytes 294944 | tf_op jit(solution)/shard_map/ppermute | solution.py:229
  37.6 2.2 join.4
  39.7 2.1 join.5
  41.9 4.2 %collective-permute-done.4.refs_2_ = bf16[144,1024]{1,0:T(8,128)(2,1)} collective-permute-done((bf16[144,1024]{1,0:T(8,128)(2,1)}, bf16[144,1024]{1,0:T(8,128)(2,1)}, u32[]{:S(2)}, u32[]{:S(2)}) %collective-permute-start.4) | collective-permute-done | bytes 294944 | tf_op jit(solution)/shard_map/ppermute | solution.py:229
  46.4 2.1 join.3
  50.0 3.8 %collective-permute-start.15 = (bf16[144,4096]{1,0:T(8,128)(2,1)S(1)}, bf16[144,4096]{1,0:T(8,128)(2,1)S(1)}, u32[]{:S(2)}, u32[]{:S(2)}) collective-permute-start(bf16[144,4096]{1,0:T(8,128)(2,1)S(1)} %broadcast_select_fusion.1), channel_id=1, source_target_pairs={{0,2},{2,4},{4,6},{6,7},{7,5},{5,3},{3,1},{1,0},{8,10},{10,12},{12... | collective-permute-start | bytes 3538952 | tf_op jit(solution)/shard_map/ppermute | solution.py:105
  58.9 20.5 %collective-permute-done.15 = bf16[144,4096]{1,0:T(8,128)(2,1)S(1)} collective-permute-done((bf16[144,4096]{1,0:T(8,128)(2,1)S(1)}, bf16[144,4096]{1,0:T(8,128)(2,1)S(1)}, u32[]{:S(2)}, u32[]{:S(2)}) %collective-permute-start.15) | collective-permute-done | bytes 1179680 | tf_op jit(solution)/shard_map/ppermute | solution.py:105
  79.6 2.5 collective-permute-start.16
  82.3 3.1 %fusion.15 = f32[288,288]{1,0:T(8,128)S(1)} fusion(bf16[288,4096]{1,0:T(8,128)(2,1)S(1)} %pad_maximum_fusion.1, bf16[144,4096]{1,0:T(8,128)(2,1)} %bitcast.2, bf16[144,4096]{1,0:T(8,128)(2,1)S(1)} %get-tuple-element.120), kind=kOutput, calls=%fused_computation.34 | convolution fusion | flops 684195840 | bytes 5050368 | tf_op jit(solution)/shard_map/dot_general | solution.py:81
  85.4 2.7 multiply_convert_fusion.1
  89.7 14.4 %collective-permute-done.16 = bf16[144,4096]{1,0:T(8,128)(2,1)S(1)} collective-permute-done((bf16[144,4096]{1,0:T(8,128)(2,1)S(1)}, bf16[144,4096]{1,0:T(8,128)(2,1)S(1)}, u32[]{:S(2)}, u32[]{:S(2)}) %collective-permute-start.16) | collective-permute-done | bytes 1179680 | tf_op jit(solution)/shard_map/ppermute | solution.py:105
  104.2 2.5 collective-permute-start.17
  106.7 8.2 %collective-permute-done.18 = bf16[144,4096]{1,0:T(8,128)(2,1)S(1)} collective-permute-done((bf16[144,4096]{1,0:T(8,128)(2,1)S(1)}, bf16[144,4096]{1,0:T(8,128)(2,1)S(1)}, u32[]{:S(2)}, u32[]{:S(2)}) %collective-permute-start.18) | collective-permute-done | bytes 1179680 | tf_op jit(solution)/shard_map/ppermute | solution.py:105
  119.8 5.1 %collective-permute-done.17 = bf16[144,4096]{1,0:T(8,128)(2,1)S(1)} collective-permute-done((bf16[144,4096]{1,0:T(8,128)(2,1)S(1)}, bf16[144,4096]{1,0:T(8,128)(2,1)S(1)}, u32[]{:S(2)}, u32[]{:S(2)}) %collective-permute-start.17) | collective-permute-done | bytes 1179680 | tf_op jit(solution)/shard_map/ppermute | solution.py:105
  126.2 2.5 collective-permute-start.21
  128.7 18.2 %collective-permute-done.19 = bf16[144,4096]{1,0:T(8,128)(2,1)S(1)} collective-permute-done((bf16[144,4096]{1,0:T(8,128)(2,1)S(1)}, bf16[144,4096]{1,0:T(8,128)(2,1)S(1)}, u32[]{:S(2)}, u32[]{:S(2)}) %collective-permute-start.19) | collective-permute-done | bytes 1179680 | tf_op jit(solution)/shard_map/ppermute | solution.py:105
  152.5 2.4 collective-permute-start.23
  154.9 19.2 %collective-permute-done.20 = bf16[144,4096]{1,0:T(8,128)(2,1)S(1)} collective-permute-done((bf16[144,4096]{1,0:T(8,128)(2,1)S(1)}, bf16[144,4096]{1,0:T(8,128)(2,1)S(1)}, u32[]{:S(2)}, u32[]{:S(2)}) %collective-permute-start.20) | collective-permute-done | bytes 1179680 | tf_op jit(solution)/shard_map/ppermute | solution.py:105
  174.7 2.7 fusion.20
  180.8 2.0 collective-permute-start.25
  182.8 17.5 %collective-permute-done.22 = bf16[144,4096]{1,0:T(8,128)(2,1)} collective-permute-done((bf16[144,4096]{1,0:T(8,128)(2,1)S(1)}, bf16[144,4096]{1,0:T(8,128)(2,1)}, u32[]{:S(2)}, u32[]{:S(2)}) %collective-permute-start.22) | collective-permute-done | bytes 1179680 | tf_op jit(solution)/shard_map/ppermute | solution.py:105
  200.3 2.7 select_select_fusion
  203.1 3.2 %broadcast_select_fusion.13 = (bf16[144,288]{1,0:T(8,128)(2,1)S(1)}, bf16[144,288]{1,0:T(8,128)(2,1)S(1)}, bf16[144,288]{1,0:T(8,128)(2,1)}, bf16[144,288]{1,0:T...) fusion(bf16[144,288]{1,0:T(8,128)(2,1)S(1)} %get-tuple-element., ...), kind=kOutput, calls=%fused_computation.129 | convolution fusion | flops 340526592 | bytes 5363713 | tf_op jit(solution)/shard_map/dot_general | solution.py:81
  208.1 2.5 convolution_convert_fusion
  212.3 3.3 %convolution_convert_fusion.2 = bf16[288,4096]{1,0:T(8,128)(2,1)S(1)} fusion(bf16[144,4096]{1,0:T(8,128)(2,1)S(1)} %get-tuple-element.117, bf16[144,4096]{1,0:T(8,128)(2,1)} %bitcast.2, bf16[144,4096]{1,0:T(8,128)(2,1)S(1)} %copy-done.13, bf16[144,4096]{1,0:T(8,128)(2,1)S(1)} %get-tuple-element.121, bf16[144,288]{1,0:T(8,128)(2,1)S(1)} %get-tuple-element.154, ...), kind=kOutput, calls=%fused_computation.4 | convolution fusion | flops 1380335616 | bytes 7409664 | tf_op jit(solution)/shard_map/dot_general | solution.py:89
  215.8 3.7 %collective-permute-start.28 = (bf16[144,4096]{1,0:T(8,128)(2,1)S(1)}, bf16[144,4096]{1,0:T(8,128)(2,1)S(1)}, u32[]{:S(2)}, u32[]{:S(2)}) collective-permute-start(bf16[144,4096]{1,0:T(8,128)(2,1)S(1)} %slice.25), channel_id=1, source_target_pairs={{0,1},{1,0},{2,3},{3,2},{4,5},{5,4},{6,7},{7,6},{8,9},{9,8},{10,11... | collective-permute-start | bytes 3538952 | tf_op jit(solution)/shard_map/ppermute | solution.py:110
  219.5 3.3 %convolution_convert_fusion.1 = bf16[288,4096]{1,0:T(8,128)(2,1)S(1)} fusion(bf16[144,4096]{1,0:T(8,128)(2,1)S(1)} %get-tuple-element.117, bf16[144,4096]{1,0:T(8,128)(2,1)} %bitcast.2, bf16[144,4096]{1,0:T(8,128)(2,1)S(1)} %copy-done.13, bf16[144,4096]{1,0:T(8,128)(2,1)S(1)} %get-tuple-element.121, bf16[144,288]{1,0:T(8,128)(2,1)S(1)} %get-tuple-element.153, ...), kind=kOutput, calls=%fused_computation.3 | convolution fusion | flops 1380335616 | bytes 7409664 | tf_op jit(solution)/shard_map/dot_general | solution.py:89
  224.4 5.8 %collective-permute-done.24 = bf16[144,4096]{1,0:T(8,128)(2,1)S(1)} collective-permute-done((bf16[144,4096]{1,0:T(8,128)(2,1)}, bf16[144,4096]{1,0:T(8,128)(2,1)S(1)}, u32[]{:S(2)}, u32[]{:S(2)}) %collective-permute-start.24) | collective-permute-done | bytes 1179680 | tf_op jit(solution)/shard_map/ppermute | solution.py:105
  230.5 2.8 %collective-permute-start.31 = (bf16[144,1024]{1,0:T(8,128)(2,1)S(1)}, bf16[144,1024]{1,0:T(8,128)(2,1)S(1)}, u32[]{:S(2)}, u32[]{:S(2)}) collective-permute-start(bf16[144,1024]{1,0:T(8,128)(2,1)S(1)} %get-tuple-element.107), channel_id=1, source_target_pairs={{0,24},{8,16},{16,8},{24,0},{1,25},{9,17},{17,9},{25,1},{2,26},{10... | collective-permute-start | bytes 884744 | tf_op jit(solution)/shard_map/ppermute | solution.py:229
  234.4 2.8 %collective-permute-start.35 = (bf16[144,1024]{1,0:T(8,128)(2,1)S(1)}, bf16[144,1024]{1,0:T(8,128)(2,1)S(1)}, u32[]{:S(2)}, u32[]{:S(2)}) collective-permute-start(bf16[144,1024]{1,0:T(8,128)(2,1)S(1)} %get-tuple-element.103), channel_id=1, source_target_pairs={{0,24},{8,16},{16,8},{24,0},{1,25},{9,17},{17,9},{25,1},{2,26},{10... | collective-permute-start | bytes 884744 | tf_op jit(solution)/shard_map/ppermute | solution.py:229
  237.5 3.9 %collective-permute-done.31.refs_3_ = bf16[144,1024]{1,0:T(8,128)(2,1)S(1)} collective-permute-done((bf16[144,1024]{1,0:T(8,128)(2,1)S(1)}, bf16[144,1024]{1,0:T(8,128)(2,1)S(1)}, u32[]{:S(2)}, u32[]{:S(2)}) %collective-permute-start.31) | collective-permute-done | bytes 294944 | tf_op jit(solution)/shard_map/ppermute | solution.py:229
  243.1 4.6 %collective-permute-done.30.refs_2_ = bf16[144,1024]{1,0:T(8,128)(2,1)S(1)} collective-permute-done((bf16[144,1024]{1,0:T(8,128)(2,1)S(1)}, bf16[144,1024]{1,0:T(8,128)(2,1)S(1)}, u32[]{:S(2)}, u32[]{:S(2)}) %collective-permute-start.30) | collective-permute-done | bytes 294944 | tf_op jit(solution)/shard_map/ppermute | solution.py:229
  247.7 2.0 collective-permute-start.27
  249.9 4.2 %collective-permute-done.35.refs_3_ = bf16[144,1024]{1,0:T(8,128)(2,1)S(1)} collective-permute-done((bf16[144,1024]{1,0:T(8,128)(2,1)S(1)}, bf16[144,1024]{1,0:T(8,128)(2,1)S(1)}, u32[]{:S(2)}, u32[]{:S(2)}) %collective-permute-start.35) | collective-permute-done | bytes 294944 | tf_op jit(solution)/shard_map/ppermute | solution.py:229
  254.0 2.7 collective-permute-start.39
  256.8 3.4 %collective-permute-done.34.refs_2_ = bf16[144,1024]{1,0:T(8,128)(2,1)S(1)} collective-permute-done((bf16[144,1024]{1,0:T(8,128)(2,1)S(1)}, bf16[144,1024]{1,0:T(8,128)(2,1)S(1)}, u32[]{:S(2)}, u32[]{:S(2)}) %collective-permute-start.34) | collective-permute-done | bytes 294944 | tf_op jit(solution)/shard_map/ppermute | solution.py:229
  262.2 2.5 fusion.16
  265.7 4.6 %adam.4 = (f32[4,144,1024]{2,1,0:T(8,128)}, f32[4,144,1024]{2,1,0:T(8,128)}, f32[4,144,1024]{2,1,0:T(8,128)}) custom-call(s32[4]{0:T(128)S(1)} %pad_add_fusion.order_ref, bf16[144,1024]{1,0:T(8,128)(2,1)S(1)} %get-tuple-element.106.refs_0_, bf16[144,1024]{1,0:T(8,128)(2,1)S(1)} %collective-permute-done.33.refs_1_, ...), custom_call_target="tpu_custom_call" | custom-call | flops 9437184 | bytes 15335424 | tf_op jit(solution)/shard_map/adam/pallas_call | solution.py:36
  270.4 4.6 %adam.3 = (f32[4,144,1024]{2,1,0:T(8,128)}, f32[4,144,1024]{2,1,0:T(8,128)}, f32[4,144,1024]{2,1,0:T(8,128)}) custom-call(s32[4]{0:T(128)S(1)} %pad_add_fusion.order_ref, bf16[144,1024]{1,0:T(8,128)(2,1)S(1)} %get-tuple-element.110.refs_0_, bf16[144,1024]{1,0:T(8,128)(2,1)S(1)} %collective-permute-done.29.refs_1_, ...), custom_call_target="tpu_custom_call" | custom-call | flops 9437184 | bytes 15335424 | tf_op jit(solution)/shard_map/adam/pallas_call | solution.py:36
  275.7 4.6 %adam.5 = (f32[4,144,1024]{2,1,0:T(8,128)}, f32[4,144,1024]{2,1,0:T(8,128)}, f32[4,144,1024]{2,1,0:T(8,128)}) custom-call(s32[4]{0:T(128)S(1)} %pad_add_fusion.order_ref, bf16[144,1024]{1,0:T(8,128)(2,1)S(1)} %get-tuple-element.102.refs_0_, bf16[144,1024]{1,0:T(8,128)(2,1)S(1)} %collective-permute-done.37.refs_1_, ...), custom_call_target="tpu_custom_call" | custom-call | flops 9437184 | bytes 15335424 | tf_op jit(solution)/shard_map/adam/pallas_call | solution.py:36
  (159 shorter events, 48.0 us)
Async XLA Ops:
  0.7 7.3 %copy-start.2 = (f32[4,144,1024]{2,1,0:T(8,128)S(1)}, f32[4,144,1024]{2,1,0:T(8,128)}, u32[]{:S(2)}) copy-start(f32[4,144,1024]{2,1,0:T(8,128)} %refs_4_.5) | copy-start | bytes 7077892
  3.4 11.8 %collective-permute-start.9 = (bf16[144,1024]{1,0:T(8,128)(2,1)S(1)}, bf16[144,1024]{1,0:T(8,128)(2,1)S(1)}, u32[]{:S(2)}, u32[]{:S(2)}) collective-permute-start(bf16[144,1024]{1,0:T(8,128)(2,1)S(1)} %get-tuple-element.95), channel_id=1, source_target_pairs={{0,24},{8,16},{16,8},{24,0},{1,25},{9,17},{17,9},{25,1},{2,26},{10... | collective-permute-start | bytes 884744 | tf_op jit(solution)/shard_map/ppermute | solution.py:229
  7.3 14.4 %collective-permute-start.8 = (bf16[144,1024]{1,0:T(8,128)(2,1)}, bf16[144,1024]{1,0:T(8,128)(2,1)}, u32[]{:S(2)}, u32[]{:S(2)}) collective-permute-start(bf16[144,1024]{1,0:T(8,128)(2,1)} %get-tuple-element.96), channel_id=1, source_target_pairs={{0,16},{8,24},{16,0},{24,8},{1,17},{9,25},{17,1},{25,9},{2,18},{10... | collective-permute-start | bytes 884744 | tf_op jit(solution)/shard_map/ppermute | solution.py:229
  7.8 9.4 %copy-start.26 = (s32[4]{0:T(128)S(1)}, s32[4]{0:T(128)}, u32[]{:S(2)}) copy-start(s32[4]{0:T(128)} %param.14) | copy-start | bytes 52
  7.9 10.0 %copy-start.1 = (f32[4,144,1024]{2,1,0:T(8,128)S(1)}, f32[4,144,1024]{2,1,0:T(8,128)}, u32[]{:S(2)}) copy-start(f32[4,144,1024]{2,1,0:T(8,128)} %refs_4_.3) | copy-start | bytes 7077892
  7.9 16.5 %collective-permute-start.7 = (bf16[144,1024]{1,0:T(8,128)(2,1)}, bf16[144,1024]{1,0:T(8,128)(2,1)}, u32[]{:S(2)}, u32[]{:S(2)}) collective-permute-start(bf16[144,1024]{1,0:T(8,128)(2,1)} %get-tuple-element.97), channel_id=1, source_target_pairs={{0,8},{8,0},{16,24},{24,16},{1,9},{9,1},{17,25},{25,17},{2,10},{10... | collective-permute-start | bytes 884744 | tf_op jit(solution)/shard_map/ppermute | solution.py:229
  8.9 19.1 %collective-permute-start.13 = (bf16[144,1024]{1,0:T(8,128)(2,1)}, bf16[144,1024]{1,0:T(8,128)(2,1)}, u32[]{:S(2)}, u32[]{:S(2)}) collective-permute-start(bf16[144,1024]{1,0:T(8,128)(2,1)} %get-tuple-element.87), channel_id=1, source_target_pairs={{0,24},{8,16},{16,8},{24,0},{1,25},{9,17},{17,9},{25,1},{2,26},{10... | collective-permute-start | bytes 884744 | tf_op jit(solution)/shard_map/ppermute | solution.py:229
  11.8 22.4 %collective-permute-start.12 = (bf16[144,1024]{1,0:T(8,128)(2,1)}, bf16[144,1024]{1,0:T(8,128)(2,1)}, u32[]{:S(2)}, u32[]{:S(2)}) collective-permute-start(bf16[144,1024]{1,0:T(8,128)(2,1)} %get-tuple-element.88), channel_id=1, source_target_pairs={{0,16},{8,24},{16,0},{24,8},{1,17},{9,25},{17,1},{25,9},{2,18},{10... | collective-permute-start | bytes 884744 | tf_op jit(solution)/shard_map/ppermute | solution.py:229
  15.2 20.9 %collective-permute-start.11 = (bf16[144,1024]{1,0:T(8,128)(2,1)}, bf16[144,1024]{1,0:T(8,128)(2,1)}, u32[]{:S(2)}, u32[]{:S(2)}) collective-permute-start(bf16[144,1024]{1,0:T(8,128)(2,1)} %get-tuple-element.89), channel_id=1, source_target_pairs={{0,8},{8,0},{16,24},{24,16},{1,9},{9,1},{17,25},{25,17},{2,10},{10... | collective-permute-start | bytes 884744 | tf_op jit(solution)/shard_map/ppermute | solution.py:229
  17.8 18.5 %copy-start.11 = (bf16[1,144,4096]{2,1,0:T(8,128)(2,1)S(1)}, bf16[1,144,4096]{2,1,0:T(8,128)(2,1)}, u32[]{:S(2)}) copy-start(bf16[1,144,4096]{2,1,0:T(8,128)(2,1)} %param.13) | copy-start | bytes 3538948
  21.7 28.1 %collective-permute-start.1 = (bf16[144,4096]{1,0:T(8,128)(2,1)}, bf16[144,4096]{1,0:T(8,128)(2,1)}, u32[]{:S(2)}, u32[]{:S(2)}) collective-permute-start(bf16[144,4096]{1,0:T(8,128)(2,1)} %bitcast.2), channel_id=1, source_target_pairs={{0,2},{2,4},{4,6},{6,7},{7,5},{5,3},{3,1},{1,0},{8,10},{10,12},{12... | collective-permute-start | bytes 3538952 | tf_op jit(solution)/shard_map/ppermute | solution.py:105
  24.4 29.4 %collective-permute-start = (bf16[144,4096]{1,0:T(8,128)(2,1)}, bf16[144,4096]{1,0:T(8,128)(2,1)}, u32[]{:S(2)}, u32[]{:S(2)}) collective-permute-start(bf16[144,4096]{1,0:T(8,128)(2,1)} %bitcast.2), channel_id=1, source_target_pairs={{2,0},{4,2},{6,4},{7,6},{5,7},{3,5},{1,3},{0,1},{10,8},{12,10},{14... | collective-permute-start | bytes 3538952 | tf_op jit(solution)/shard_map/ppermute | solution.py:105
  28.0 13.8 %collective-permute-start.5 = (bf16[144,1024]{1,0:T(8,128)(2,1)}, bf16[144,1024]{1,0:T(8,128)(2,1)}, u32[]{:S(2)}, u32[]{:S(2)}) collective-permute-start(bf16[144,1024]{1,0:T(8,128)(2,1)} %get-tuple-element.91), channel_id=1, source_target_pairs={{0,24},{8,16},{16,8},{24,0},{1,25},{9,17},{17,9},{25,1},{2,26},{10... | collective-permute-start | bytes 884744 | tf_op jit(solution)/shard_map/ppermute | solution.py:229
  34.2 12.0 %collective-permute-start.4 = (bf16[144,1024]{1,0:T(8,128)(2,1)}, bf16[144,1024]{1,0:T(8,128)(2,1)}, u32[]{:S(2)}, u32[]{:S(2)}) collective-permute-start(bf16[144,1024]{1,0:T(8,128)(2,1)} %get-tuple-element.92), channel_id=1, source_target_pairs={{0,16},{8,24},{16,0},{24,8},{1,17},{9,25},{17,1},{25,9},{2,18},{10... | collective-permute-start | bytes 884744 | tf_op jit(solution)/shard_map/ppermute | solution.py:229
  36.2 10.2 %collective-permute-start.3 = (bf16[144,1024]{1,0:T(8,128)(2,1)}, bf16[144,1024]{1,0:T(8,128)(2,1)}, u32[]{:S(2)}, u32[]{:S(2)}) collective-permute-start(bf16[144,1024]{1,0:T(8,128)(2,1)} %get-tuple-element.93), channel_id=1, source_target_pairs={{0,8},{8,0},{16,24},{24,16},{1,9},{9,1},{17,25},{25,17},{2,10},{10... | collective-permute-start | bytes 884744 | tf_op jit(solution)/shard_map/ppermute | solution.py:229
  41.9 13.4 %collective-permute-start.14 = (bf16[144,4096]{1,0:T(8,128)(2,1)S(1)}, bf16[144,4096]{1,0:T(8,128)(2,1)S(1)}, u32[]{:S(2)}, u32[]{:S(2)}) collective-permute-start(bf16[144,4096]{1,0:T(8,128)(2,1)S(1)} %join.5), channel_id=1, source_target_pairs={{0,1},{1,0},{2,3},{3,2},{4,5},{5,4},{6,7},{7,6},{8,9},{9,8},{10,11... | collective-permute-start | bytes 3538952 | tf_op jit(solution)/shard_map/ppermute | solution.py:110
  46.1 9.4 %collective-permute-start.10 = (bf16[144,4096]{1,0:T(8,128)(2,1)S(1)}, bf16[144,4096]{1,0:T(8,128)(2,1)S(1)}, u32[]{:S(2)}, u32[]{:S(2)}) collective-permute-start(bf16[144,4096]{1,0:T(8,128)(2,1)S(1)} %join.4), channel_id=1, source_target_pairs={{0,1},{1,0},{2,3},{3,2},{4,5},{5,4},{6,7},{7,6},{8,9},{9,8},{10,11... | collective-permute-start | bytes 3538952 | tf_op jit(solution)/shard_map/ppermute | solution.py:110
  48.5 7.2 %collective-permute-start.6 = (bf16[144,4096]{1,0:T(8,128)(2,1)S(1)}, bf16[144,4096]{1,0:T(8,128)(2,1)S(1)}, u32[]{:S(2)}, u32[]{:S(2)}) collective-permute-start(bf16[144,4096]{1,0:T(8,128)(2,1)S(1)} %join.3), channel_id=1, source_target_pairs={{0,1},{1,0},{2,3},{3,2},{4,5},{5,4},{6,7},{7,6},{8,9},{9,8},{10,11... | collective-permute-start | bytes 3538952 | tf_op jit(solution)/shard_map/ppermute | solution.py:110
  50.0 29.5 %collective-permute-start.15 = (bf16[144,4096]{1,0:T(8,128)(2,1)S(1)}, bf16[144,4096]{1,0:T(8,128)(2,1)S(1)}, u32[]{:S(2)}, u32[]{:S(2)}) collective-permute-start(bf16[144,4096]{1,0:T(8,128)(2,1)S(1)} %broadcast_select_fusion.1), channel_id=1, source_target_pairs={{0,2},{2,4},{4,6},{6,7},{7,5},{5,3},{3,1},{1,0},{8,10},{10,12},{12... | collective-permute-start | bytes 3538952 | tf_op jit(solution)/shard_map/ppermute | solution.py:105
  55.2 26.9 %collective-permute-start.2 = (bf16[144,4096]{1,0:T(8,128)(2,1)S(1)}, bf16[144,4096]{1,0:T(8,128)(2,1)S(1)}, u32[]{:S(2)}, u32[]{:S(2)}) collective-permute-start(bf16[144,4096]{1,0:T(8,128)(2,1)S(1)} %get-tuple-element.122), channel_id=1, source_target_pairs={{2,0},{4,2},{6,4},{7,6},{5,7},{3,5},{1,3},{0,1},{10,8},{12,10},{14... | collective-permute-start | bytes 3538952 | tf_op jit(solution)/shard_map/ppermute | solution.py:105
  57.0 90.4 %copy-start.18 = (f32[144,288]{1,0:T(8,128)}, f32[144,288]{1,0:T(8,128)S(1)}, u32[]{:S(2)}) copy-start(f32[144,288]{1,0:T(8,128)S(1)} %fusion.62) | copy-start | bytes 497668
  58.1 89.2 %copy-start.21 = (f32[144,288]{1,0:T(8,128)}, f32[144,288]{1,0:T(8,128)S(1)}, u32[]{:S(2)}) copy-start(f32[144,288]{1,0:T(8,128)S(1)} %get-tuple-element.150) | copy-start | bytes 497668
  79.6 24.5 %collective-permute-start.16 = (bf16[144,4096]{1,0:T(8,128)(2,1)S(1)}, bf16[144,4096]{1,0:T(8,128)(2,1)S(1)}, u32[]{:S(2)}, u32[]{:S(2)}) collective-permute-start(bf16[144,4096]{1,0:T(8,128)(2,1)S(1)} %broadcast_select_fusion), channel_id=1, source_target_pairs={{0,2},{2,4},{4,6},{6,7},{7,5},{5,3},{3,1},{1,0},{8,10},{10,12},{12... | collective-permute-start | bytes 3538952 | tf_op jit(solution)/shard_map/ppermute | solution.py:105
  88.1 26.8 %collective-permute-start.18 = (bf16[144,4096]{1,0:T(8,128)(2,1)S(1)}, bf16[144,4096]{1,0:T(8,128)(2,1)S(1)}, u32[]{:S(2)}, u32[]{:S(2)}) collective-permute-start(bf16[144,4096]{1,0:T(8,128)(2,1)S(1)} %get-tuple-element.119), channel_id=1, source_target_pairs={{2,0},{4,2},{6,4},{7,6},{5,7},{3,5},{1,3},{0,1},{10,8},{12,10},{14... | collective-permute-start | bytes 3538952 | tf_op jit(solution)/shard_map/ppermute | solution.py:105
  104.2 20.7 %collective-permute-start.17 = (bf16[144,4096]{1,0:T(8,128)(2,1)S(1)}, bf16[144,4096]{1,0:T(8,128)(2,1)S(1)}, u32[]{:S(2)}, u32[]{:S(2)}) collective-permute-start(bf16[144,4096]{1,0:T(8,128)(2,1)S(1)} %select_select_fusion.5), channel_id=1, source_target_pairs={{0,2},{2,4},{4,6},{6,7},{7,5},{5,3},{3,1},{1,0},{8,10},{10,12},{12... | collective-permute-start | bytes 3538952 | tf_op jit(solution)/shard_map/ppermute | solution.py:105
  119.1 27.8 %collective-permute-start.19 = (bf16[144,4096]{1,0:T(8,128)(2,1)S(1)}, bf16[144,4096]{1,0:T(8,128)(2,1)S(1)}, u32[]{:S(2)}, u32[]{:S(2)}) collective-permute-start(bf16[144,4096]{1,0:T(8,128)(2,1)S(1)} %get-tuple-element.118), channel_id=1, source_target_pairs={{2,0},{4,2},{6,4},{7,6},{5,7},{3,5},{1,3},{0,1},{10,8},{12,10},{14... | collective-permute-start | bytes 3538952 | tf_op jit(solution)/shard_map/ppermute | solution.py:105
  126.2 26.0 %collective-permute-start.21 = (bf16[144,4096]{1,0:T(8,128)(2,1)}, bf16[144,4096]{1,0:T(8,128)(2,1)S(1)}, u32[]{:S(2)}, u32[]{:S(2)}) collective-permute-start(bf16[144,4096]{1,0:T(8,128)(2,1)} %select_add_fusion.7), channel_id=1, source_target_pairs={{0,2},{2,4},{4,6},{6,7},{7,5},{5,3},{3,1},{1,0},{8,10},{10,12},{12... | collective-permute-start | bytes 3538952 | tf_op jit(solution)/shard_map/ppermute | solution.py:105
  147.3 26.7 %collective-permute-start.20 = (bf16[144,4096]{1,0:T(8,128)(2,1)S(1)}, bf16[144,4096]{1,0:T(8,128)(2,1)S(1)}, u32[]{:S(2)}, u32[]{:S(2)}) collective-permute-start(bf16[144,4096]{1,0:T(8,128)(2,1)S(1)} %get-tuple-element.116), channel_id=1, source_target_pairs={{2,0},{4,2},{6,4},{7,6},{5,7},{3,5},{1,3},{0,1},{10,8},{12,10},{14... | collective-permute-start | bytes 3538952 | tf_op jit(solution)/shard_map/ppermute | solution.py:105
  149.4 53.7 %copy-start.14 = (bf16[144,288]{1,0:T(8,128)(2,1)}, bf16[144,288]{1,0:T(8,128)(2,1)S(1)}, u32[]{:S(2)}) copy-start(bf16[144,288]{1,0:T(8,128)(2,1)S(1)} %get-tuple-element.132) | copy-start | bytes 248836
  152.5 28.0 %collective-permute-start.23 = (bf16[144,4096]{1,0:T(8,128)(2,1)S(1)}, bf16[144,4096]{1,0:T(8,128)(2,1)S(1)}, u32[]{:S(2)}, u32[]{:S(2)}) collective-permute-start(bf16[144,4096]{1,0:T(8,128)(2,1)S(1)} %select_add_fusion.5), channel_id=1, source_target_pairs={{0,2},{2,4},{4,6},{6,7},{7,5},{5,3},{3,1},{1,0},{8,10},{10,12},{12... | collective-permute-start | bytes 3538952 | tf_op jit(solution)/shard_map/ppermute | solution.py:105
  174.6 25.7 %collective-permute-start.22 = (bf16[144,4096]{1,0:T(8,128)(2,1)S(1)}, bf16[144,4096]{1,0:T(8,128)(2,1)}, u32[]{:S(2)}, u32[]{:S(2)}) collective-permute-start(bf16[144,4096]{1,0:T(8,128)(2,1)S(1)} %get-tuple-element.114), channel_id=1, source_target_pairs={{2,0},{4,2},{6,4},{7,6},{5,7},{3,5},{1,3},{0,1},{10,8},{12,10},{14... | collective-permute-start | bytes 3538952 | tf_op jit(solution)/shard_map/ppermute | solution.py:105
  180.8 43.1 %collective-permute-start.25 = (bf16[144,4096]{1,0:T(8,128)(2,1)S(1)}, bf16[144,4096]{1,0:T(8,128)(2,1)S(1)}, u32[]{:S(2)}, u32[]{:S(2)}) collective-permute-start(bf16[144,4096]{1,0:T(8,128)(2,1)S(1)} %select_add_fusion.3), channel_id=1, source_target_pairs={{0,2},{2,4},{4,6},{6,7},{7,5},{5,3},{3,1},{1,0},{8,10},{10,12},{12... | collective-permute-start | bytes 3538952 | tf_op jit(solution)/shard_map/ppermute | solution.py:105
  211.7 25.6 %collective-permute-start.36 = (bf16[144,4096]{1,0:T(8,128)(2,1)}, bf16[144,4096]{1,0:T(8,128)(2,1)S(1)}, u32[]{:S(2)}, u32[]{:S(2)}) collective-permute-start(bf16[144,4096]{1,0:T(8,128)(2,1)} %slice.29), channel_id=1, source_target_pairs={{0,1},{1,0},{2,3},{3,2},{4,5},{5,4},{6,7},{7,6},{8,9},{9,8},{10,11... | collective-permute-start | bytes 3538952 | tf_op jit(solution)/shard_map/ppermute | solution.py:110
  211.7 18.4 %collective-permute-start.24 = (bf16[144,4096]{1,0:T(8,128)(2,1)}, bf16[144,4096]{1,0:T(8,128)(2,1)S(1)}, u32[]{:S(2)}, u32[]{:S(2)}) collective-permute-start(bf16[144,4096]{1,0:T(8,128)(2,1)} %get-tuple-element.112), channel_id=1, source_target_pairs={{2,0},{4,2},{6,4},{7,6},{5,7},{3,5},{1,3},{0,1},{10,8},{12,10},{14... | collective-permute-start | bytes 3538952 | tf_op jit(solution)/shard_map/ppermute | solution.py:105
  215.8 8.3 %collective-permute-start.28 = (bf16[144,4096]{1,0:T(8,128)(2,1)S(1)}, bf16[144,4096]{1,0:T(8,128)(2,1)S(1)}, u32[]{:S(2)}, u32[]{:S(2)}) collective-permute-start(bf16[144,4096]{1,0:T(8,128)(2,1)S(1)} %slice.25), channel_id=1, source_target_pairs={{0,1},{1,0},{2,3},{3,2},{4,5},{5,4},{6,7},{7,6},{8,9},{9,8},{10,11... | collective-permute-start | bytes 3538952 | tf_op jit(solution)/shard_map/ppermute | solution.py:110
  223.0 11.0 %collective-permute-start.32 = (bf16[144,4096]{1,0:T(8,128)(2,1)S(1)}, bf16[144,4096]{1,0:T(8,128)(2,1)S(1)}, u32[]{:S(2)}, u32[]{:S(2)}) collective-permute-start(bf16[144,4096]{1,0:T(8,128)(2,1)S(1)} %slice.27), channel_id=1, source_target_pairs={{0,1},{1,0},{2,3},{3,2},{4,5},{5,4},{6,7},{7,6},{8,9},{9,8},{10,11... | collective-permute-start | bytes 3538952 | tf_op jit(solution)/shard_map/ppermute | solution.py:110
  230.5 10.9 %collective-permute-start.31 = (bf16[144,1024]{1,0:T(8,128)(2,1)S(1)}, bf16[144,1024]{1,0:T(8,128)(2,1)S(1)}, u32[]{:S(2)}, u32[]{:S(2)}) collective-permute-start(bf16[144,1024]{1,0:T(8,128)(2,1)S(1)} %get-tuple-element.107), channel_id=1, source_target_pairs={{0,24},{8,16},{16,8},{24,0},{1,25},{9,17},{17,9},{25,1},{2,26},{10... | collective-permute-start | bytes 884744 | tf_op jit(solution)/shard_map/ppermute | solution.py:229
  233.3 14.4 %collective-permute-start.30 = (bf16[144,1024]{1,0:T(8,128)(2,1)S(1)}, bf16[144,1024]{1,0:T(8,128)(2,1)S(1)}, u32[]{:S(2)}, u32[]{:S(2)}) collective-permute-start(bf16[144,1024]{1,0:T(8,128)(2,1)S(1)} %get-tuple-element.108), channel_id=1, source_target_pairs={{0,16},{8,24},{16,0},{24,8},{1,17},{9,25},{17,1},{25,9},{2,18},{10... | collective-permute-start | bytes 884744 | tf_op jit(solution)/shard_map/ppermute | solution.py:229
  233.5 16.3 %collective-permute-start.29 = (bf16[144,1024]{1,0:T(8,128)(2,1)S(1)}, bf16[144,1024]{1,0:T(8,128)(2,1)S(1)}, u32[]{:S(2)}, u32[]{:S(2)}) collective-permute-start(bf16[144,1024]{1,0:T(8,128)(2,1)S(1)} %get-tuple-element.109), channel_id=1, source_target_pairs={{0,8},{8,0},{16,24},{24,16},{1,9},{9,1},{17,25},{25,17},{2,10},{10... | collective-permute-start | bytes 884744 | tf_op jit(solution)/shard_map/ppermute | solution.py:229
  234.4 19.6 %collective-permute-start.35 = (bf16[144,1024]{1,0:T(8,128)(2,1)S(1)}, bf16[144,1024]{1,0:T(8,128)(2,1)S(1)}, u32[]{:S(2)}, u32[]{:S(2)}) collective-permute-start(bf16[144,1024]{1,0:T(8,128)(2,1)S(1)} %get-tuple-element.103), channel_id=1, source_target_pairs={{0,24},{8,16},{16,8},{24,0},{1,25},{9,17},{17,9},{25,1},{2,26},{10... | collective-permute-start | bytes 884744 | tf_op jit(solution)/shard_map/ppermute | solution.py:229
  237.3 22.9 %collective-permute-start.34 = (bf16[144,1024]{1,0:T(8,128)(2,1)S(1)}, bf16[144,1024]{1,0:T(8,128)(2,1)S(1)}, u32[]{:S(2)}, u32[]{:S(2)}) collective-permute-start(bf16[144,1024]{1,0:T(8,128)(2,1)S(1)} %get-tuple-element.104), channel_id=1, source_target_pairs={{0,16},{8,24},{16,0},{24,8},{1,17},{9,25},{17,1},{25,9},{2,18},{10... | collective-permute-start | bytes 884744 | tf_op jit(solution)/shard_map/ppermute | solution.py:229
  241.4 20.4 %collective-permute-start.33 = (bf16[144,1024]{1,0:T(8,128)(2,1)S(1)}, bf16[144,1024]{1,0:T(8,128)(2,1)S(1)}, u32[]{:S(2)}, u32[]{:S(2)}) collective-permute-start(bf16[144,1024]{1,0:T(8,128)(2,1)S(1)} %get-tuple-element.105), channel_id=1, source_target_pairs={{0,8},{8,0},{16,24},{24,16},{1,9},{9,1},{17,25},{25,17},{2,10},{10... | collective-permute-start | bytes 884744 | tf_op jit(solution)/shard_map/ppermute | solution.py:229
  247.7 32.6 %collective-permute-start.27 = (bf16[144,4096]{1,0:T(8,128)(2,1)S(1)}, bf16[144,4096]{1,0:T(8,128)(2,1)S(1)}, u32[]{:S(2)}, u32[]{:S(2)}) collective-permute-start(bf16[144,4096]{1,0:T(8,128)(2,1)S(1)} %select_add_fusion.1), channel_id=1, source_target_pairs={{0,2},{2,4},{4,6},{6,7},{7,5},{5,3},{3,1},{1,0},{8,10},{10,12},{12... | collective-permute-start | bytes 3538952 | tf_op jit(solution)/shard_map/ppermute | solution.py:105
  249.8 30.6 %collective-permute-start.26 = (bf16[144,4096]{1,0:T(8,128)(2,1)S(1)}, bf16[144,4096]{1,0:T(8,128)(2,1)S(1)}, u32[]{:S(2)}, u32[]{:S(2)}) collective-permute-start(bf16[144,4096]{1,0:T(8,128)(2,1)S(1)} %select_add_fusion), channel_id=1, source_target_pairs={{2,0},{4,2},{6,4},{7,6},{5,7},{3,5},{1,3},{0,1},{10,8},{12,10},{14... | collective-permute-start | bytes 3538952 | tf_op jit(solution)/shard_map/ppermute | solution.py:105
  254.0 21.0 %collective-permute-start.39 = (bf16[144,1024]{1,0:T(8,128)(2,1)S(1)}, bf16[144,1024]{1,0:T(8,128)(2,1)S(1)}, u32[]{:S(2)}, u32[]{:S(2)}) collective-permute-start(bf16[144,1024]{1,0:T(8,128)(2,1)S(1)} %get-tuple-element.99), channel_id=1, source_target_pairs={{0,24},{8,16},{16,8},{24,0},{1,25},{9,17},{17,9},{25,1},{2,26},{10... | collective-permute-start | bytes 884744 | tf_op jit(solution)/shard_map/ppermute | solution.py:229
  260.2 14.8 %collective-permute-start.38 = (bf16[144,1024]{1,0:T(8,128)(2,1)S(1)}, bf16[144,1024]{1,0:T(8,128)(2,1)S(1)}, u32[]{:S(2)}, u32[]{:S(2)}) collective-permute-start(bf16[144,1024]{1,0:T(8,128)(2,1)S(1)} %get-tuple-element.100), channel_id=1, source_target_pairs={{0,16},{8,24},{16,0},{24,8},{1,17},{9,25},{17,1},{25,9},{2,18},{10... | collective-permute-start | bytes 884744 | tf_op jit(solution)/shard_map/ppermute | solution.py:229
  261.7 13.3 %collective-permute-start.37 = (bf16[144,1024]{1,0:T(8,128)(2,1)S(1)}, bf16[144,1024]{1,0:T(8,128)(2,1)S(1)}, u32[]{:S(2)}, u32[]{:S(2)}) collective-permute-start(bf16[144,1024]{1,0:T(8,128)(2,1)S(1)} %get-tuple-element.101), channel_id=1, source_target_pairs={{0,8},{8,0},{16,24},{24,16},{1,9},{9,1},{17,25},{25,17},{2,10},{10... | collective-permute-start | bytes 884744 | tf_op jit(solution)/shard_map/ppermute | solution.py:229
  270.4 5.4 %copy-start.9 = (f32[4,144,1024]{2,1,0:T(8,128)S(1)}, f32[4,144,1024]{2,1,0:T(8,128)}, u32[]{:S(2)}) copy-start(f32[4,144,1024]{2,1,0:T(8,128)} %refs_6_.5) | copy-start | bytes 7077892
  (22 other events, 59.5 us)
where the time goes:
time: 283 us; the launch traced here: 282 us
  waiting for transfers between devices  144 us (51%)
  starting transfers between devices  53.1 us (19%)
  matrix products  36.4 us (13%)
  Pallas kernels  20.2 us (7%)
  other arithmetic  17.2 us (6%)
  local copies, waits for them, and re-layouts  9.36 us (3%)
    ppermute x16, waiting for transfers between devices, hop(): return lax.ppermute(value, 'cuts', pairs)  111 us
    ppermute x18, waiting for transfers between devices, trade(): lax.ppermute(pieces[turn], 'expert', [(e, partner(e, turn, experts)) for...  33.3 us
    ppermute x18, starting transfers between devices, trade(): lax.ppermute(pieces[turn], 'expert', [(e, partner(e, turn, experts)) for...  27.7 us
    ppermute x16, starting transfers between devices, hop(): return lax.ppermute(value, 'cuts', pairs)  20.4 us
    dot_general x9, matrix products, dot_t(): lax.dot_general(a, b, (((1,), (1,)), ((), ())), preferred_element_type=jn...  18.1 us
    pallas_call x3, Pallas kernels, adam_update(): pl.pallas_call(functools.partial(adam_kernel, count), grid_spec=pltpu.Pre...  13.9 us
    dot_general x9, matrix products, dot_n(): lax.dot_general(a, b, (((1,), (0,)), ((), ())), preferred_element_type=jn...  9.19 us
    dot_general x3, matrix products, dot_0(): lax.dot_general(a, b, (((0,), (0,)), ((), ())), preferred_element_type=jn...  9.14 us
  transfers between devices with their start and end apart: 40, of which 20 were waited for; matrix products, arithmetic and copies ran while one was open for 20% of the time, Pallas kernels for 7%

commit v1 on v0

--- a/solution.py
+++ b/solution.py
@@ -87,6 +87,9 @@
 
 def dot_0(a, b):
     return lax.dot_general(a, b, (((0,), (0,)), ((), ())), preferred_element_type=jnp.float32)
+
+
+STREAMS = 2
 
 
 def device_at(core, place, chips):
@@ -216,8 +219,14 @@
         own_row = jnp.arange(local_rows, dtype=jnp.int32) + cut * local_rows
         keep = (own_row < live)[:, None]
         own_t = token_rows[0]
-        own_c = jnp.where(keep, cotangent[0], jnp.zeros_like(cotangent[0]))
-        own_c = lax.optimization_barrier(own_c)
+        own_c = cotangent[0]
+
+        def live_rows(blocks):
+            block = jnp.int32(0)
+            for p, b in blocks.items():
+                block = jnp.where(place == p, b, block)
+            owner = jnp.where(core == 0, 2 * block, 2 * (chips - 1 - block) + 1)
+            return (jnp.arange(local_rows, dtype=jnp.int32) + owner * local_rows < live)[:, None]
 
         me = lax.axis_index("expert")
         cols = gate_master.shape[2]
@@ -248,14 +257,22 @@
             hidden = (gate_pre * jax.nn.sigmoid(gate_pre) * up_pre).astype(jnp.bfloat16)
             return gate_pre, up_pre, hidden, dot_n(hidden, down_w).astype(jnp.bfloat16)
 
-        def backward(block, gate_pre, up_pre):
-            grad_hidden = dot_t(block, down_w)
+        def backward(block, alive, gate_pre, up_pre):
+            grad_hidden = jnp.where(alive, dot_t(block, down_w), 0.0)
             sig = jax.nn.sigmoid(gate_pre)
             d_gate = (grad_hidden * up_pre * sig * (1.0 + gate_pre * (1.0 - sig))).astype(jnp.bfloat16)
             d_up = (grad_hidden * (gate_pre * sig)).astype(jnp.bfloat16)
             return d_gate, d_up, (dot_n(d_gate, gate_w) + dot_n(d_up, up_w)).astype(jnp.bfloat16)
 
-        arrays = {("own", "T"): own_t, ("own", "C"): own_c}
+        whole = {("own", "T"): own_t, ("own", "C"): own_c}
+        arrays = {}
+
+        def part(name, q):
+            if (name, q) not in arrays:
+                width = whole[name].shape[1] // STREAMS
+                arrays[name, q] = lax.slice_in_dim(whole[name], q * width, (q + 1) * width, axis=1)
+            return arrays[name, q]
+
         t_work, c_work, t_got, c_got = [], [], {}, {}
         own_places = {p: p for p in range(chips)}
         t_steps = [i for i, work in enumerate(works) if any(k == "T" for k, _ in work)]
@@ -276,34 +293,40 @@
 
         last_sent = own_t
         for step, (sent, work) in enumerate(zip(sends, works)):
-            for d in (1, -1):
-                before = ("got", d, step - 1)
-                if before in arrays:
-                    arrays[before] = lax.optimization_barrier((arrays[before], last_sent))[0]
-                firsts = {p: arrays[terms[0]] for (e, p), (_, terms) in sent.items() if e == d}
-                if not firsts:
-                    continue
-                value = pick(place, firsts, None)
-                seconds = {p: arrays[terms[1]] for (e, p), (_, terms) in sent.items() if e == d and terms[1]}
-                if seconds:
-                    more = pick(place, seconds, None)
-                    here = jnp.zeros((), jnp.bool_)
-                    for p in seconds:
-                        here = here | (place == p)
-                    more = jnp.where(here, more, jnp.zeros_like(more))
-                    value = value + more
-                last_sent = value
-                came_in = hop(value, d, chips)
-                arrays["got", d, step] = came_in
+            for q in range(STREAMS):
+                for d in (1, -1):
+                    before = (("got", d, step - 1), q)
+                    if before in arrays:
+                        arrays[before] = lax.optimization_barrier((arrays[before], last_sent))[0]
+                    firsts = {p: part(terms[0], q) for (e, p), (_, terms) in sent.items() if e == d}
+                    if not firsts:
+                        continue
+                    value = pick(place, firsts, None)
+                    seconds = {p: part(terms[1], q) for (e, p), (_, terms) in sent.items() if e == d and terms[1]}
+                    if seconds:
+                        more = pick(place, seconds, None)
+                        here = jnp.zeros((), jnp.bool_)
+                        for p in seconds:
+                            here = here | (place == p)
+                        more = jnp.where(here, more, jnp.zeros_like(more))
+                        value = value + more
+                    last_sent = value
+                    arrays[("got", d, step), q] = hop(value, d, chips)
             for kind in "TC":
                 blocks = {p: b for (k, p), (b, _) in work.items() if k == kind}
                 if not blocks:
                     continue
-                block = pick(place, {p: arrays[name] for (k, p), (_, name) in work.items() if k == kind}, None)
+                names = {p: name for (k, p), (_, name) in work.items() if k == kind}
+                block = jnp.concatenate(
+                    [pick(place, {p: part(name, q) for p, name in names.items()}, None) for q in range(STREAMS)],
+                    axis=1,
+                )
+                if STREAMS > 1:
+                    block = lax.optimization_barrier(block)
                 with_own = own_with[kind] == step
                 batch = [(step, blocks, block)]
                 if with_own:
-                    batch.append(("own", own_places, arrays["own", kind]))
+                    batch.append(("own", own_places, whole["own", kind]))
                 joined = jnp.concatenate([entry[2] for entry in batch], axis=0)
                 if kind == "T":
                     results = forward(joined)
@@ -312,29 +335,27 @@
                         jnp.concatenate([of_block(entry[1], t_work, t_got, item) for entry in batch], axis=0)
                         for item in (1, 2)
                     ]
-                    results = backward(joined, *pres)
+                    alive = jnp.concatenate([live_rows(entry[1]) for entry in batch], axis=0)
+                    results = backward(joined, alive, *pres)
                 results = [jnp.split(value, len(batch), axis=0) for value in results]
                 for i, (name, its_blocks, its_block) in enumerate(batch):
                     mine = [value[i] for value in results]
                     mine[-1] = lax.optimization_barrier(mine[-1])
                     (t_work if kind == "T" else c_work).append((name, its_blocks))
                     (t_got if kind == "T" else c_got)[name] = (its_block, *mine)
-                    arrays["made", kind, name] = mine[-1]
-
-        def total(own, kind):
-            result = lax.optimization_barrier((own, last_sent))[0].astype(jnp.float32)
+                    whole["made", kind, name] = mine[-1]
+
+        def total(kind, q):
+            result = lax.optimization_barrier((part(("made", {"O": "T", "I": "C"}[kind], "own"), q), last_sent))[0]
+            result = result.astype(jnp.float32)
             ends = {p: [came[d][p][kind, p] for d in (1, -1) if (kind, p) in came[d][p]] for p in range(chips)}
             for turn in range(2):
-                terms = {p: arrays[names[turn]] for p, names in ends.items() if len(names) > turn}
-                if not terms:
+                late = {}
+                for name in dict.fromkeys(names[turn] for names in ends.values() if len(names) > turn):
+                    value = lax.optimization_barrier((part(name, q), last_sent))[0]
+                    late.update({p: value for p, names in ends.items() if names[turn:turn + 1] == [name]})
+                if not late:
                     continue
-                uses = {}
-                for p, value in terms.items():
-                    uses.setdefault(id(value), (value, []))[1].append(p)
-                late = {}
-                for value, places in uses.values():
-                    value = lax.optimization_barrier((value, last_sent))[0]
-                    late.update({p: value for p in places})
                 more = pick(place, late, None)
                 if len(late) < chips:
                     here = jnp.zeros((), jnp.bool_)
@@ -344,12 +365,15 @@
                 result = result + more.astype(jnp.float32)
             return result
 
-        out_rows = jnp.where(keep, total(arrays["made", "T", "own"], "O"), 0.0).astype(jnp.bfloat16)[None]
-        input_grads = total(arrays["made", "C", "own"], "I").astype(jnp.bfloat16)[None]
+        outs = [jnp.where(keep, total("O", q), 0.0).astype(jnp.bfloat16) for q in range(STREAMS)]
+        out_rows = jnp.concatenate(outs, axis=1)[None]
+        backs = [total("I", q).astype(jnp.bfloat16) for q in range(STREAMS)]
+        input_grads = jnp.concatenate(backs, axis=1)[None]
 
         tokens = jnp.concatenate([t_got[name][0] for name, _ in t_work], axis=0)
         upstream = jnp.concatenate([c_got[name][0] for name, _ in c_work], axis=0)
-        hidden = jnp.concatenate([of_block(blocks, t_work, t_got, 3) for _, blocks in c_work], axis=0)
+        hidden = [jnp.where(live_rows(blocks), of_block(blocks, t_work, t_got, 3), 0) for _, blocks in c_work]
+        hidden = jnp.concatenate(hidden, axis=0)
         d_gate = jnp.concatenate([of_block(blocks, c_work, c_got, 1) for _, blocks in t_work], axis=0)
         d_up = jnp.concatenate([of_block(blocks, c_work, c_got, 2) for _, blocks in t_work], axis=0)
 

time: 283 us -> 294 us (1.039)
  waiting for transfers between devices: 144 us -> 153 us
  starting transfers between devices: 53.1 us -> 61.4 us
  matrix products: 36.4 us -> 28.6 us
  other arithmetic: 17.2 us -> 20.7 us
    ppermute x16 -> x32, starting transfers between devices: 20.4 us -> 34.3 us  [hop(): return lax.ppermute(value, 'cuts', pairs)]
    dot_general x9, matrix products: 18.1 us -> 12.5 us  [dot_t(): lax.dot_general(a, b, (((1,), (1,)), ((), ())), preferred_element_type=jn...]
    ppermute x18, waiting for transfers between devices: 33.3 us -> 38.8 us  [trade(): lax.ppermute(pieces[turn], 'expert', [(e, partner(e, turn, experts)) for...]
    ppermute x16 -> x32, waiting for transfers between devices: 111 us -> 114 us  [hop(): return lax.ppermute(value, 'cuts', pairs)]
    ppermute x6, starting transfers between devices: 5.03 us -> 1.78 us  [swap_cores(): return lax.ppermute(value, 'cuts', pairs)]
    select_n x12 -> x20, other arithmetic: 7.66 us -> 6.86 us  [pick(): result = jnp.where(here, value, result)]
  transfers between devices with their start and end apart: 40 -> 56, of which waited for: 20 -> 27; matrix products, arithmetic and copies ran while one was open for 20% -> 18% of each run, Pallas kernels for 7% -> 5%
where the time goes in v1:
time: 294 us
  waiting for transfers between devices  153 us (52%)
  starting transfers between devices  61.4 us (21%)
  matrix products  28.6 us (10%)
  other arithmetic  20.7 us (7%)
  Pallas kernels  18.7 us (6%)
  local copies, waits for them, and re-layouts  9.18 us (3%)
    ppermute x32, waiting for transfers between devices, hop(): return lax.ppermute(value, 'cuts', pairs)  114 us
    ppermute x18, waiting for transfers between devices, trade(): lax.ppermute(pieces[turn], 'expert', [(e, partner(e, turn, experts)) for...  38.8 us
    ppermute x32, starting transfers between devices, hop(): return lax.ppermute(value, 'cuts', pairs)  34.3 us
    ppermute x18, starting transfers between devices, trade(): lax.ppermute(pieces[turn], 'expert', [(e, partner(e, turn, experts)) for...  25.3 us
    pallas_call x3, Pallas kernels, adam_update(): pl.pallas_call(functools.partial(adam_kernel, count), grid_spec=pltpu.Pre...  13.8 us
    dot_general x9, matrix products, dot_t(): lax.dot_general(a, b, (((1,), (1,)), ((), ())), preferred_element_type=jn...  12.5 us
    dot_general x9, matrix products, dot_n(): lax.dot_general(a, b, (((1,), (0,)), ((), ())), preferred_element_type=jn...  9.12 us
    dot_general x3, matrix products, dot_0(): lax.dot_general(a, b, (((0,), (0,)), ((), ())), preferred_element_type=jn...  6.99 us
  transfers between devices with their start and end apart: 56, of which 27 were waited for; matrix products, arithmetic and copies ran while one was open for 18% of the time, Pallas kernels for 5%

profile of v1, /device:TPU:0, one launch (start us, length us, event | category | flops | bytes accessed | tf_op | source)
XLA Modules:
  0.0 293.6 jit_solution(11156894584038342260)
XLA Ops:
  0.7 2.7 fusion.46
  3.4 3.9 %collective-permute-start.7 = (bf16[144,1024]{1,0:T(8,128)(2,1)}, bf16[144,1024]{1,0:T(8,128)(2,1)S(1)}, u32[]{:S(2)}, u32[]{:S(2)}) collective-permute-start(bf16[144,1024]{1,0:T(8,128)(2,1)} %get-tuple-element.139), channel_id=1, source_target_pairs={{0,24},{8,16},{16,8},{24,0},{1,25},{9,17},{17,9},{25,1},{2,26},{10... | collective-permute-start | bytes 884744 | tf_op jit(solution)/shard_map/ppermute | solution.py:238
  8.9 2.9 collective-permute-start.15
  15.5 2.1 collective-permute-start.1
  17.7 4.2 %collective-permute-done.6.refs_2_ = bf16[144,1024]{1,0:T(8,128)(2,1)S(1)} collective-permute-done((bf16[144,1024]{1,0:T(8,128)(2,1)}, bf16[144,1024]{1,0:T(8,128)(2,1)S(1)}, u32[]{:S(2)}, u32[]{:S(2)}) %collective-permute-start.6) | collective-permute-done | bytes 294944 | tf_op jit(solution)/shard_map/ppermute | solution.py:238
  26.0 2.2 collective-permute-done.15.refs_3_
  30.2 4.3 %collective-permute-done.14.refs_2_ = bf16[144,1024]{1,0:T(8,128)(2,1)} collective-permute-done((bf16[144,1024]{1,0:T(8,128)(2,1)}, bf16[144,1024]{1,0:T(8,128)(2,1)}, u32[]{:S(2)}, u32[]{:S(2)}) %collective-permute-start.14) | collective-permute-done | bytes 294944 | tf_op jit(solution)/shard_map/ppermute | solution.py:238
  39.8 2.0 join.5
  41.9 2.0 collective-permute-start.4
  43.9 2.2 collective-permute-done.10.refs_2_
  50.3 4.9 %collective-permute-done.4 = bf16[144,2048]{1,0:T(8,128)(2,1)S(1)} collective-permute-done((bf16[144,2048]{1,0:T(8,128)(2,1)S(1)}, bf16[144,2048]{1,0:T(8,128)(2,1)S(1)}, u32[]{:S(2)}, u32[]{:S(2)}) %collective-permute-start.4) | collective-permute-done | bytes 589856 | tf_op jit(solution)/shard_map/ppermute | solution.py:108
  55.2 2.5 collective-permute-start.17
  57.7 2.6 collective-permute-done.3
  62.2 2.9 collective-permute-done.17
  72.5 9.2 %collective-permute-done.2 = bf16[144,2048]{1,0:T(8,128)(2,1)S(1)} collective-permute-done((bf16[144,2048]{1,0:T(8,128)(2,1)S(1)}, bf16[144,2048]{1,0:T(8,128)(2,1)S(1)}, u32[]{:S(2)}, u32[]{:S(2)}) %collective-permute-start.2) | collective-permute-done | bytes 589856 | tf_op jit(solution)/shard_map/ppermute | solution.py:108
  82.0 2.0 collective-permute-start.23
  84.0 10.3 %collective-permute-done.18 = bf16[144,2048]{1,0:T(8,128)(2,1)S(1)} collective-permute-done((bf16[144,2048]{1,0:T(8,128)(2,1)S(1)}, bf16[144,2048]{1,0:T(8,128)(2,1)S(1)}, u32[]{:S(2)}, u32[]{:S(2)}) %collective-permute-start.18) | collective-permute-done | bytes 589856 | tf_op jit(solution)/shard_map/ppermute | solution.py:108
  99.3 2.0 collective-permute-start.21
  101.3 4.5 %collective-permute-done.24 = bf16[144,2048]{1,0:T(8,128)(2,1)S(1)} collective-permute-done((bf16[144,2048]{1,0:T(8,128)(2,1)S(1)}, bf16[144,2048]{1,0:T(8,128)(2,1)S(1)}, u32[]{:S(2)}, u32[]{:S(2)}) %collective-permute-start.24) | collective-permute-done | bytes 589856 | tf_op jit(solution)/shard_map/ppermute | solution.py:108
  106.1 2.0 collective-permute-start.28
  108.1 10.3 %collective-permute-done.22 = bf16[144,2048]{1,0:T(8,128)(2,1)S(1)} collective-permute-done((bf16[144,2048]{1,0:T(8,128)(2,1)S(1)}, bf16[144,2048]{1,0:T(8,128)(2,1)S(1)}, u32[]{:S(2)}, u32[]{:S(2)}) %collective-permute-start.22) | collective-permute-done | bytes 589856 | tf_op jit(solution)/shard_map/ppermute | solution.py:108
  123.3 2.0 collective-permute-start.29
  125.4 5.8 %collective-permute-done.25 = bf16[144,2048]{1,0:T(8,128)(2,1)S(1)} collective-permute-done((bf16[144,2048]{1,0:T(8,128)(2,1)S(1)}, bf16[144,2048]{1,0:T(8,128)(2,1)S(1)}, u32[]{:S(2)}, u32[]{:S(2)}) %collective-permute-start.25) | collective-permute-done | bytes 589856 | tf_op jit(solution)/shard_map/ppermute | solution.py:108
  131.5 2.0 collective-permute-start.31
  133.5 10.2 %collective-permute-done.27 = bf16[144,2048]{1,0:T(8,128)(2,1)S(1)} collective-permute-done((bf16[144,2048]{1,0:T(8,128)(2,1)S(1)}, bf16[144,2048]{1,0:T(8,128)(2,1)S(1)}, u32[]{:S(2)}, u32[]{:S(2)}) %collective-permute-start.27) | collective-permute-done | bytes 589856 | tf_op jit(solution)/shard_map/ppermute | solution.py:108
  149.3 7.1 %collective-permute-done.26 = bf16[144,2048]{1,0:T(8,128)(2,1)S(1)} collective-permute-done((bf16[144,2048]{1,0:T(8,128)(2,1)S(1)}, bf16[144,2048]{1,0:T(8,128)(2,1)S(1)}, u32[]{:S(2)}, u32[]{:S(2)}) %collective-permute-start.26) | collective-permute-done | bytes 589856 | tf_op jit(solution)/shard_map/ppermute | solution.py:108
  157.7 2.0 collective-permute-start.35
  159.7 9.4 %collective-permute-done.30 = bf16[144,2048]{1,0:T(8,128)(2,1)S(1)} collective-permute-done((bf16[144,2048]{1,0:T(8,128)(2,1)S(1)}, bf16[144,2048]{1,0:T(8,128)(2,1)S(1)}, u32[]{:S(2)}, u32[]{:S(2)}) %collective-permute-start.30) | collective-permute-done | bytes 589856 | tf_op jit(solution)/shard_map/ppermute | solution.py:108
  176.0 2.0 collective-permute-start.39
  178.0 3.7 %collective-permute-done.32 = bf16[144,2048]{1,0:T(8,128)(2,1)S(1)} collective-permute-done((bf16[144,2048]{1,0:T(8,128)(2,1)S(1)}, bf16[144,2048]{1,0:T(8,128)(2,1)S(1)}, u32[]{:S(2)}, u32[]{:S(2)}) %collective-permute-start.32) | collective-permute-done | bytes 589856 | tf_op jit(solution)/shard_map/ppermute | solution.py:108
  183.7 2.0 collective-permute-start.37
  185.7 8.7 %collective-permute-done.34 = bf16[144,2048]{1,0:T(8,128)(2,1)} collective-permute-done((bf16[144,2048]{1,0:T(8,128)(2,1)}, bf16[144,2048]{1,0:T(8,128)(2,1)}, u32[]{:S(2)}, u32[]{:S(2)}) %collective-permute-start.34) | collective-permute-done | bytes 589856 | tf_op jit(solution)/shard_map/ppermute | solution.py:108
  194.4 2.1 select_select_fusion
  200.7 2.3 convolution_convert_fusion
  203.0 2.3 convolution_convert_fusion.2
  205.3 2.5 convolution_convert_fusion.1
  210.2 2.1 collective-permute-done.36
  212.4 2.0 collective-permute-start.43
  214.4 2.0 collective-permute-start.41
  219.4 9.1 %collective-permute-done.42 = bf16[144,2048]{1,0:T(8,128)(2,1)S(1)} collective-permute-done((bf16[144,2048]{1,0:T(8,128)(2,1)S(1)}, bf16[144,2048]{1,0:T(8,128)(2,1)S(1)}, u32[]{:S(2)}, u32[]{:S(2)}) %collective-permute-start.42) | collective-permute-done | bytes 589856 | tf_op jit(solution)/shard_map/ppermute | solution.py:108
  229.1 12.0 %collective-permute-done.40 = bf16[144,2048]{1,0:T(8,128)(2,1)S(1)} collective-permute-done((bf16[144,2048]{1,0:T(8,128)(2,1)S(1)}, bf16[144,2048]{1,0:T(8,128)(2,1)S(1)}, u32[]{:S(2)}, u32[]{:S(2)}) %collective-permute-start.40) | collective-permute-done | bytes 589856 | tf_op jit(solution)/shard_map/ppermute | solution.py:108
  249.6 3.5 %collective-permute-done.47.refs_3_ = bf16[144,1024]{1,0:T(8,128)(2,1)S(1)} collective-permute-done((bf16[144,1024]{1,0:T(8,128)(2,1)S(1)}, bf16[144,1024]{1,0:T(8,128)(2,1)S(1)}, u32[]{:S(2)}, u32[]{:S(2)}) %collective-permute-start.47) | collective-permute-done | bytes 294944 | tf_op jit(solution)/shard_map/ppermute | solution.py:238
  254.3 5.1 %collective-permute-done.51.refs_3_ = bf16[144,1024]{1,0:T(8,128)(2,1)S(1)} collective-permute-done((bf16[144,1024]{1,0:T(8,128)(2,1)S(1)}, bf16[144,1024]{1,0:T(8,128)(2,1)S(1)}, u32[]{:S(2)}, u32[]{:S(2)}) %collective-permute-start.51) | collective-permute-done | bytes 294944 | tf_op jit(solution)/shard_map/ppermute | solution.py:238
  259.3 6.4 %collective-permute-done.50.refs_2_ = bf16[144,1024]{1,0:T(8,128)(2,1)S(1)} collective-permute-done((bf16[144,1024]{1,0:T(8,128)(2,1)S(1)}, bf16[144,1024]{1,0:T(8,128)(2,1)S(1)}, u32[]{:S(2)}, u32[]{:S(2)}) %collective-permute-start.50) | collective-permute-done | bytes 294944 | tf_op jit(solution)/shard_map/ppermute | solution.py:238
  269.0 4.6 %adam.4 = (f32[4,144,1024]{2,1,0:T(8,128)}, f32[4,144,1024]{2,1,0:T(8,128)}, f32[4,144,1024]{2,1,0:T(8,128)}) custom-call(s32[4]{0:T(128)S(1)} %pad_add_fusion.order_ref, bf16[144,1024]{1,0:T(8,128)(2,1)S(1)} %get-tuple-element.154.refs_0_, bf16[144,1024]{1,0:T(8,128)(2,1)S(1)} %collective-permute-done.49.refs_1_, ...), custom_call_target="tpu_custom_call" | custom-call | flops 9437184 | bytes 15335424 | tf_op jit(solution)/shard_map/adam/pallas_call | solution.py:36
  273.6 10.0 %collective-permute-done.46.refs_2_ = bf16[144,1024]{1,0:T(8,128)(2,1)S(1)} collective-permute-done((bf16[144,1024]{1,0:T(8,128)(2,1)S(1)}, bf16[144,1024]{1,0:T(8,128)(2,1)S(1)}, u32[]{:S(2)}, u32[]{:S(2)}) %collective-permute-start.46) | collective-permute-done | bytes 294944 | tf_op jit(solution)/shard_map/ppermute | solution.py:238
  283.7 4.6 %adam.3 = (f32[4,144,1024]{2,1,0:T(8,128)}, f32[4,144,1024]{2,1,0:T(8,128)}, f32[4,144,1024]{2,1,0:T(8,128)}) custom-call(s32[4]{0:T(128)S(1)} %pad_add_fusion.order_ref, bf16[144,1024]{1,0:T(8,128)(2,1)S(1)} %get-tuple-element.158.refs_0_, bf16[144,1024]{1,0:T(8,128)(2,1)S(1)} %collective-permute-done.45.refs_1_, ...), custom_call_target="tpu_custom_call" | custom-call | flops 9437184 | bytes 15335424 | tf_op jit(solution)/shard_map/adam/pallas_call | solution.py:36
  289.0 4.6 %adam.5 = (f32[4,144,1024]{2,1,0:T(8,128)}, f32[4,144,1024]{2,1,0:T(8,128)}, f32[4,144,1024]{2,1,0:T(8,128)}) custom-call(s32[4]{0:T(128)S(1)} %pad_add_fusion.order_ref, bf16[144,1024]{1,0:T(8,128)(2,1)S(1)} %get-tuple-element.150.refs_0_, bf16[144,1024]{1,0:T(8,128)(2,1)S(1)} %collective-permute-done.53.refs_1_, ...), custom_call_target="tpu_custom_call" | custom-call | flops 9437184 | bytes 15335424 | tf_op jit(solution)/shard_map/adam/pallas_call | solution.py:36
  (238 shorter events, 79.6 us)
Async XLA Ops:
  7.3 14.5 %collective-permute-start.6 = (bf16[144,1024]{1,0:T(8,128)(2,1)}, bf16[144,1024]{1,0:T(8,128)(2,1)S(1)}, u32[]{:S(2)}, u32[]{:S(2)}) collective-permute-start(bf16[144,1024]{1,0:T(8,128)(2,1)} %get-tuple-element.140), channel_id=1, source_target_pairs={{0,16},{8,24},{16,0},{24,8},{1,17},{9,25},{17,1},{25,9},{2,18},{10... | collective-permute-start | bytes 884744 | tf_op jit(solution)/shard_map/ppermute | solution.py:238
  7.9 16.6 %collective-permute-start.5 = (bf16[144,1024]{1,0:T(8,128)(2,1)}, bf16[144,1024]{1,0:T(8,128)(2,1)}, u32[]{:S(2)}, u32[]{:S(2)}) collective-permute-start(bf16[144,1024]{1,0:T(8,128)(2,1)} %get-tuple-element.141), channel_id=1, source_target_pairs={{0,8},{8,0},{16,24},{24,16},{1,9},{9,1},{17,25},{25,17},{2,10},{10... | collective-permute-start | bytes 884744 | tf_op jit(solution)/shard_map/ppermute | solution.py:238
  8.9 19.3 %collective-permute-start.15 = (bf16[144,1024]{1,0:T(8,128)(2,1)}, bf16[144,1024]{1,0:T(8,128)(2,1)}, u32[]{:S(2)}, u32[]{:S(2)}) collective-permute-start(bf16[144,1024]{1,0:T(8,128)(2,1)} %get-tuple-element.135), channel_id=1, source_target_pairs={{0,24},{8,16},{16,8},{24,0},{1,25},{9,17},{17,9},{25,1},{2,26},{10... | collective-permute-start | bytes 884744 | tf_op jit(solution)/shard_map/ppermute | solution.py:238
  11.8 22.8 %collective-permute-start.14 = (bf16[144,1024]{1,0:T(8,128)(2,1)}, bf16[144,1024]{1,0:T(8,128)(2,1)}, u32[]{:S(2)}, u32[]{:S(2)}) collective-permute-start(bf16[144,1024]{1,0:T(8,128)(2,1)} %get-tuple-element.136), channel_id=1, source_target_pairs={{0,16},{8,24},{16,0},{24,8},{1,17},{9,25},{17,1},{25,9},{2,18},{10... | collective-permute-start | bytes 884744 | tf_op jit(solution)/shard_map/ppermute | solution.py:238
  15.5 33.2 %collective-permute-start.1 = (bf16[144,2048]{1,0:T(8,128)(2,1)}, bf16[144,2048]{1,0:T(8,128)(2,1)S(1)}, u32[]{:S(2)}, u32[]{:S(2)}) collective-permute-start(bf16[144,2048]{1,0:T(8,128)(2,1)} %get-tuple-element.163), channel_id=1, source_target_pairs={{0,2},{2,4},{4,6},{6,7},{7,5},{5,3},{3,1},{1,0},{8,10},{10,12},{12... | collective-permute-start | bytes 1769480 | tf_op jit(solution)/shard_map/ppermute | solution.py:108
  21.8 16.0 %collective-permute-start.13 = (bf16[144,1024]{1,0:T(8,128)(2,1)S(1)}, bf16[144,1024]{1,0:T(8,128)(2,1)S(1)}, u32[]{:S(2)}, u32[]{:S(2)}) collective-permute-start(bf16[144,1024]{1,0:T(8,128)(2,1)S(1)} %copy-done.25), channel_id=1, source_target_pairs={{0,8},{8,0},{16,24},{24,16},{1,9},{9,1},{17,25},{25,17},{2,10},{10... | collective-permute-start | bytes 884744 | tf_op jit(solution)/shard_map/ppermute | solution.py:238
  24.5 17.4 %collective-permute-start.11 = (bf16[144,1024]{1,0:T(8,128)(2,1)S(1)}, bf16[144,1024]{1,0:T(8,128)(2,1)S(1)}, u32[]{:S(2)}, u32[]{:S(2)}) collective-permute-start(bf16[144,1024]{1,0:T(8,128)(2,1)S(1)} %get-tuple-element.143), channel_id=1, source_target_pairs={{0,24},{8,16},{16,8},{24,0},{1,25},{9,17},{17,9},{25,1},{2,26},{10... | collective-permute-start | bytes 884744 | tf_op jit(solution)/shard_map/ppermute | solution.py:238
  28.2 17.9 %collective-permute-start.10 = (bf16[144,1024]{1,0:T(8,128)(2,1)S(1)}, bf16[144,1024]{1,0:T(8,128)(2,1)S(1)}, u32[]{:S(2)}, u32[]{:S(2)}) collective-permute-start(bf16[144,1024]{1,0:T(8,128)(2,1)S(1)} %get-tuple-element.144), channel_id=1, source_target_pairs={{0,16},{8,24},{16,0},{24,8},{1,17},{9,25},{17,1},{25,9},{2,18},{10... | collective-permute-start | bytes 884744 | tf_op jit(solution)/shard_map/ppermute | solution.py:238
  46.5 20.2 %collective-permute-start.16 = (bf16[144,4096]{1,0:T(8,128)(2,1)S(1)}, bf16[144,4096]{1,0:T(8,128)(2,1)S(1)}, u32[]{:S(2)}, u32[]{:S(2)}) collective-permute-start(bf16[144,4096]{1,0:T(8,128)(2,1)S(1)} %join.5), channel_id=1, source_target_pairs={{0,1},{1,0},{2,3},{3,2},{4,5},{5,4},{6,7},{7,6},{8,9},{9,8},{10,11... | collective-permute-start | bytes 3538952 | tf_op jit(solution)/shard_map/ppermute | solution.py:113
  48.7 19.9 %collective-permute-start.12 = (bf16[144,4096]{1,0:T(8,128)(2,1)S(1)}, bf16[144,4096]{1,0:T(8,128)(2,1)S(1)}, u32[]{:S(2)}, u32[]{:S(2)}) collective-permute-start(bf16[144,4096]{1,0:T(8,128)(2,1)S(1)} %join.4), channel_id=1, source_target_pairs={{0,1},{1,0},{2,3},{3,2},{4,5},{5,4},{6,7},{7,6},{8,9},{9,8},{10,11... | collective-permute-start | bytes 3538952 | tf_op jit(solution)/shard_map/ppermute | solution.py:113
  50.2 18.6 %collective-permute-start.8 = (bf16[144,4096]{1,0:T(8,128)(2,1)S(1)}, bf16[144,4096]{1,0:T(8,128)(2,1)S(1)}, u32[]{:S(2)}, u32[]{:S(2)}) collective-permute-start(bf16[144,4096]{1,0:T(8,128)(2,1)S(1)} %join.3), channel_id=1, source_target_pairs={{0,1},{1,0},{2,3},{3,2},{4,5},{5,4},{6,7},{7,6},{8,9},{9,8},{10,11... | collective-permute-start | bytes 3538952 | tf_op jit(solution)/shard_map/ppermute | solution.py:113
  60.4 21.5 %collective-permute-start.19 = (bf16[144,2048]{1,0:T(8,128)(2,1)S(1)}, bf16[144,2048]{1,0:T(8,128)(2,1)S(1)}, u32[]{:S(2)}, u32[]{:S(2)}) collective-permute-start(bf16[144,2048]{1,0:T(8,128)(2,1)S(1)} %broadcast_select_fusion.2), channel_id=1, source_target_pairs={{0,2},{2,4},{4,6},{6,7},{7,5},{5,3},{3,1},{1,0},{8,10},{10,12},{12... | collective-permute-start | bytes 1769480 | tf_op jit(solution)/shard_map/ppermute | solution.py:108
  65.1 16.7 %collective-permute-start.2 = (bf16[144,2048]{1,0:T(8,128)(2,1)S(1)}, bf16[144,2048]{1,0:T(8,128)(2,1)S(1)}, u32[]{:S(2)}, u32[]{:S(2)}) collective-permute-start(bf16[144,2048]{1,0:T(8,128)(2,1)S(1)} %get-tuple-element.192), channel_id=1, source_target_pairs={{2,0},{4,2},{6,4},{7,6},{5,7},{3,5},{1,3},{0,1},{10,8},{12,10},{14... | collective-permute-start | bytes 1769480 | tf_op jit(solution)/shard_map/ppermute | solution.py:108
  66.7 27.6 %collective-permute-start.18 = (bf16[144,2048]{1,0:T(8,128)(2,1)S(1)}, bf16[144,2048]{1,0:T(8,128)(2,1)S(1)}, u32[]{:S(2)}, u32[]{:S(2)}) collective-permute-start(bf16[144,2048]{1,0:T(8,128)(2,1)S(1)} %get-tuple-element.194), channel_id=1, source_target_pairs={{2,0},{4,2},{6,4},{7,6},{5,7},{3,5},{1,3},{0,1},{10,8},{12,10},{14... | collective-permute-start | bytes 1769480 | tf_op jit(solution)/shard_map/ppermute | solution.py:108
  72.1 27.1 %collective-permute-start.20 = (bf16[144,2048]{1,0:T(8,128)(2,1)S(1)}, bf16[144,2048]{1,0:T(8,128)(2,1)S(1)}, u32[]{:S(2)}, u32[]{:S(2)}) collective-permute-start(bf16[144,2048]{1,0:T(8,128)(2,1)S(1)} %broadcast_select_fusion.1), channel_id=1, source_target_pairs={{0,2},{2,4},{4,6},{6,7},{7,5},{5,3},{3,1},{1,0},{8,10},{10,12},{12... | collective-permute-start | bytes 1769480 | tf_op jit(solution)/shard_map/ppermute | solution.py:108
  81.9 24.0 %collective-permute-start.24 = (bf16[144,2048]{1,0:T(8,128)(2,1)S(1)}, bf16[144,2048]{1,0:T(8,128)(2,1)S(1)}, u32[]{:S(2)}, u32[]{:S(2)}) collective-permute-start(bf16[144,2048]{1,0:T(8,128)(2,1)S(1)} %get-tuple-element.190), channel_id=1, source_target_pairs={{2,0},{4,2},{6,4},{7,6},{5,7},{3,5},{1,3},{0,1},{10,8},{12,10},{14... | collective-permute-start | bytes 1769480 | tf_op jit(solution)/shard_map/ppermute | solution.py:108
  82.0 24.0 %collective-permute-start.23 = (bf16[144,2048]{1,0:T(8,128)(2,1)S(1)}, bf16[144,2048]{1,0:T(8,128)(2,1)S(1)}, u32[]{:S(2)}, u32[]{:S(2)}) collective-permute-start(bf16[144,2048]{1,0:T(8,128)(2,1)S(1)} %broadcast_select_fusion), channel_id=1, source_target_pairs={{0,2},{2,4},{4,6},{6,7},{7,5},{5,3},{3,1},{1,0},{8,10},{10,12},{12... | collective-permute-start | bytes 1769480 | tf_op jit(solution)/shard_map/ppermute | solution.py:108
  96.0 22.5 %collective-permute-start.22 = (bf16[144,2048]{1,0:T(8,128)(2,1)S(1)}, bf16[144,2048]{1,0:T(8,128)(2,1)S(1)}, u32[]{:S(2)}, u32[]{:S(2)}) collective-permute-start(bf16[144,2048]{1,0:T(8,128)(2,1)S(1)} %get-tuple-element.187), channel_id=1, source_target_pairs={{2,0},{4,2},{6,4},{7,6},{5,7},{3,5},{1,3},{0,1},{10,8},{12,10},{14... | collective-permute-start | bytes 1769480 | tf_op jit(solution)/shard_map/ppermute | solution.py:108
  99.3 23.9 %collective-permute-start.21 = (bf16[144,2048]{1,0:T(8,128)(2,1)S(1)}, bf16[144,2048]{1,0:T(8,128)(2,1)S(1)}, u32[]{:S(2)}, u32[]{:S(2)}) collective-permute-start(bf16[144,2048]{1,0:T(8,128)(2,1)S(1)} %select_select_fusion.11), channel_id=1, source_target_pairs={{0,2},{2,4},{4,6},{6,7},{7,5},{5,3},{3,1},{1,0},{8,10},{10,12},{12... | collective-permute-start | bytes 1769480 | tf_op jit(solution)/shard_map/ppermute | solution.py:108
  106.0 25.1 %collective-permute-start.25 = (bf16[144,2048]{1,0:T(8,128)(2,1)S(1)}, bf16[144,2048]{1,0:T(8,128)(2,1)S(1)}, u32[]{:S(2)}, u32[]{:S(2)}) collective-permute-start(bf16[144,2048]{1,0:T(8,128)(2,1)S(1)} %get-tuple-element.184), channel_id=1, source_target_pairs={{2,0},{4,2},{6,4},{7,6},{5,7},{3,5},{1,3},{0,1},{10,8},{12,10},{14... | collective-permute-start | bytes 1769480 | tf_op jit(solution)/shard_map/ppermute | solution.py:108
  106.1 25.2 %collective-permute-start.28 = (bf16[144,2048]{1,0:T(8,128)(2,1)S(1)}, bf16[144,2048]{1,0:T(8,128)(2,1)S(1)}, u32[]{:S(2)}, u32[]{:S(2)}) collective-permute-start(bf16[144,2048]{1,0:T(8,128)(2,1)S(1)} %select_select_fusion.9), channel_id=1, source_target_pairs={{0,2},{2,4},{4,6},{6,7},{7,5},{5,3},{3,1},{1,0},{8,10},{10,12},{12... | collective-permute-start | bytes 1769480 | tf_op jit(solution)/shard_map/ppermute | solution.py:108
  123.2 20.6 %collective-permute-start.27 = (bf16[144,2048]{1,0:T(8,128)(2,1)S(1)}, bf16[144,2048]{1,0:T(8,128)(2,1)S(1)}, u32[]{:S(2)}, u32[]{:S(2)}) collective-permute-start(bf16[144,2048]{1,0:T(8,128)(2,1)S(1)} %get-tuple-element.186), channel_id=1, source_target_pairs={{2,0},{4,2},{6,4},{7,6},{5,7},{3,5},{1,3},{0,1},{10,8},{12,10},{14... | collective-permute-start | bytes 1769480 | tf_op jit(solution)/shard_map/ppermute | solution.py:108
  123.3 23.8 %collective-permute-start.29 = (bf16[144,2048]{1,0:T(8,128)(2,1)S(1)}, bf16[144,2048]{1,0:T(8,128)(2,1)S(1)}, u32[]{:S(2)}, u32[]{:S(2)}) collective-permute-start(bf16[144,2048]{1,0:T(8,128)(2,1)S(1)} %select_add_fusion.15), channel_id=1, source_target_pairs={{0,2},{2,4},{4,6},{6,7},{7,5},{5,3},{3,1},{1,0},{8,10},{10,12},{12... | collective-permute-start | bytes 1769480 | tf_op jit(solution)/shard_map/ppermute | solution.py:108
  131.3 25.1 %collective-permute-start.26 = (bf16[144,2048]{1,0:T(8,128)(2,1)S(1)}, bf16[144,2048]{1,0:T(8,128)(2,1)S(1)}, u32[]{:S(2)}, u32[]{:S(2)}) collective-permute-start(bf16[144,2048]{1,0:T(8,128)(2,1)S(1)} %get-tuple-element.180), channel_id=1, source_target_pairs={{2,0},{4,2},{6,4},{7,6},{5,7},{3,5},{1,3},{0,1},{10,8},{12,10},{14... | collective-permute-start | bytes 1769480 | tf_op jit(solution)/shard_map/ppermute | solution.py:108
  131.5 25.2 %collective-permute-start.31 = (bf16[144,2048]{1,0:T(8,128)(2,1)S(1)}, bf16[144,2048]{1,0:T(8,128)(2,1)S(1)}, u32[]{:S(2)}, u32[]{:S(2)}) collective-permute-start(bf16[144,2048]{1,0:T(8,128)(2,1)S(1)} %select_add_fusion.13), channel_id=1, source_target_pairs={{0,2},{2,4},{4,6},{6,7},{7,5},{5,3},{3,1},{1,0},{8,10},{10,12},{12... | collective-permute-start | bytes 1769480 | tf_op jit(solution)/shard_map/ppermute | solution.py:108
  144.1 25.0 %collective-permute-start.30 = (bf16[144,2048]{1,0:T(8,128)(2,1)S(1)}, bf16[144,2048]{1,0:T(8,128)(2,1)S(1)}, u32[]{:S(2)}, u32[]{:S(2)}) collective-permute-start(bf16[144,2048]{1,0:T(8,128)(2,1)S(1)} %get-tuple-element.182), channel_id=1, source_target_pairs={{2,0},{4,2},{6,4},{7,6},{5,7},{3,5},{1,3},{0,1},{10,8},{12,10},{14... | collective-permute-start | bytes 1769480 | tf_op jit(solution)/shard_map/ppermute | solution.py:108
  147.3 27.8 %collective-permute-start.33 = (bf16[144,2048]{1,0:T(8,128)(2,1)S(1)}, bf16[144,2048]{1,0:T(8,128)(2,1)S(1)}, u32[]{:S(2)}, u32[]{:S(2)}) collective-permute-start(bf16[144,2048]{1,0:T(8,128)(2,1)S(1)} %select_add_fusion.11), channel_id=1, source_target_pairs={{0,2},{2,4},{4,6},{6,7},{7,5},{5,3},{3,1},{1,0},{8,10},{10,12},{12... | collective-permute-start | bytes 1769480 | tf_op jit(solution)/shard_map/ppermute | solution.py:108
  156.7 25.0 %collective-permute-start.32 = (bf16[144,2048]{1,0:T(8,128)(2,1)S(1)}, bf16[144,2048]{1,0:T(8,128)(2,1)S(1)}, u32[]{:S(2)}, u32[]{:S(2)}) collective-permute-start(bf16[144,2048]{1,0:T(8,128)(2,1)S(1)} %get-tuple-element.176), channel_id=1, source_target_pairs={{2,0},{4,2},{6,4},{7,6},{5,7},{3,5},{1,3},{0,1},{10,8},{12,10},{14... | collective-permute-start | bytes 1769480 | tf_op jit(solution)/shard_map/ppermute | solution.py:108
  157.7 25.1 %collective-permute-start.35 = (bf16[144,2048]{1,0:T(8,128)(2,1)}, bf16[144,2048]{1,0:T(8,128)(2,1)S(1)}, u32[]{:S(2)}, u32[]{:S(2)}) collective-permute-start(bf16[144,2048]{1,0:T(8,128)(2,1)} %select_add_fusion.9), channel_id=1, source_target_pairs={{0,2},{2,4},{4,6},{6,7},{7,5},{5,3},{3,1},{1,0},{8,10},{10,12},{12... | collective-permute-start | bytes 1769480 | tf_op jit(solution)/shard_map/ppermute | solution.py:108
  170.2 24.2 %collective-permute-start.34 = (bf16[144,2048]{1,0:T(8,128)(2,1)}, bf16[144,2048]{1,0:T(8,128)(2,1)}, u32[]{:S(2)}, u32[]{:S(2)}) collective-permute-start(bf16[144,2048]{1,0:T(8,128)(2,1)} %get-tuple-element.178), channel_id=1, source_target_pairs={{2,0},{4,2},{6,4},{7,6},{5,7},{3,5},{1,3},{0,1},{10,8},{12,10},{14... | collective-permute-start | bytes 1769480 | tf_op jit(solution)/shard_map/ppermute | solution.py:108
  176.0 33.9 %collective-permute-start.39 = (bf16[144,2048]{1,0:T(8,128)(2,1)}, bf16[144,2048]{1,0:T(8,128)(2,1)S(1)}, u32[]{:S(2)}, u32[]{:S(2)}) collective-permute-start(bf16[144,2048]{1,0:T(8,128)(2,1)} %select_add_fusion.7), channel_id=1, source_target_pairs={{0,2},{2,4},{4,6},{6,7},{7,5},{5,3},{3,1},{1,0},{8,10},{10,12},{12... | collective-permute-start | bytes 1769480 | tf_op jit(solution)/shard_map/ppermute | solution.py:108
  182.7 27.3 %collective-permute-start.38 = (bf16[144,2048]{1,0:T(8,128)(2,1)}, bf16[144,2048]{1,0:T(8,128)(2,1)S(1)}, u32[]{:S(2)}, u32[]{:S(2)}) collective-permute-start(bf16[144,2048]{1,0:T(8,128)(2,1)} %get-tuple-element.172), channel_id=1, source_target_pairs={{2,0},{4,2},{6,4},{7,6},{5,7},{3,5},{1,3},{0,1},{10,8},{12,10},{14... | collective-permute-start | bytes 1769480 | tf_op jit(solution)/shard_map/ppermute | solution.py:108
  183.7 26.4 %collective-permute-start.37 = (bf16[144,2048]{1,0:T(8,128)(2,1)}, bf16[144,2048]{1,0:T(8,128)(2,1)S(1)}, u32[]{:S(2)}, u32[]{:S(2)}) collective-permute-start(bf16[144,2048]{1,0:T(8,128)(2,1)} %select_add_fusion.5), channel_id=1, source_target_pairs={{0,2},{2,4},{4,6},{6,7},{7,5},{5,3},{3,1},{1,0},{8,10},{10,12},{12... | collective-permute-start | bytes 1769480 | tf_op jit(solution)/shard_map/ppermute | solution.py:108
  209.8 31.9 %collective-permute-start.44 = (bf16[144,4096]{1,0:T(8,128)(2,1)S(1)}, bf16[144,4096]{1,0:T(8,128)(2,1)S(1)}, u32[]{:S(2)}, u32[]{:S(2)}) collective-permute-start(bf16[144,4096]{1,0:T(8,128)(2,1)S(1)} %slice.125), channel_id=1, source_target_pairs={{0,1},{1,0},{2,3},{3,2},{4,5},{5,4},{6,7},{7,6},{8,9},{9,8},{10,11... | collective-permute-start | bytes 3538952 | tf_op jit(solution)/shard_map/ppermute | solution.py:113
  212.4 16.2 %collective-permute-start.42 = (bf16[144,2048]{1,0:T(8,128)(2,1)S(1)}, bf16[144,2048]{1,0:T(8,128)(2,1)S(1)}, u32[]{:S(2)}, u32[]{:S(2)}) collective-permute-start(bf16[144,2048]{1,0:T(8,128)(2,1)S(1)} %select_add_fusion), channel_id=1, source_target_pairs={{2,0},{4,2},{6,4},{7,6},{5,7},{3,5},{1,3},{0,1},{10,8},{12,10},{14... | collective-permute-start | bytes 1769480 | tf_op jit(solution)/shard_map/ppermute | solution.py:108
  212.4 16.2 %collective-permute-start.43 = (bf16[144,2048]{1,0:T(8,128)(2,1)S(1)}, bf16[144,2048]{1,0:T(8,128)(2,1)S(1)}, u32[]{:S(2)}, u32[]{:S(2)}) collective-permute-start(bf16[144,2048]{1,0:T(8,128)(2,1)S(1)} %select_add_fusion.1), channel_id=1, source_target_pairs={{0,2},{2,4},{4,6},{6,7},{7,5},{5,3},{3,1},{1,0},{8,10},{10,12},{12... | collective-permute-start | bytes 1769480 | tf_op jit(solution)/shard_map/ppermute | solution.py:108
  214.4 26.7 %collective-permute-start.40 = (bf16[144,2048]{1,0:T(8,128)(2,1)S(1)}, bf16[144,2048]{1,0:T(8,128)(2,1)S(1)}, u32[]{:S(2)}, u32[]{:S(2)}) collective-permute-start(bf16[144,2048]{1,0:T(8,128)(2,1)S(1)} %select_add_fusion.2), channel_id=1, source_target_pairs={{2,0},{4,2},{6,4},{7,6},{5,7},{3,5},{1,3},{0,1},{10,8},{12,10},{14... | collective-permute-start | bytes 1769480 | tf_op jit(solution)/shard_map/ppermute | solution.py:108
  214.4 26.7 %collective-permute-start.41 = (bf16[144,2048]{1,0:T(8,128)(2,1)S(1)}, bf16[144,2048]{1,0:T(8,128)(2,1)S(1)}, u32[]{:S(2)}, u32[]{:S(2)}) collective-permute-start(bf16[144,2048]{1,0:T(8,128)(2,1)S(1)} %select_add_fusion.3), channel_id=1, source_target_pairs={{0,2},{2,4},{4,6},{6,7},{7,5},{5,3},{3,1},{1,0},{8,10},{10,12},{12... | collective-permute-start | bytes 1769480 | tf_op jit(solution)/shard_map/ppermute | solution.py:108
  228.6 19.1 %collective-permute-start.52 = (bf16[144,4096]{1,0:T(8,128)(2,1)S(1)}, bf16[144,4096]{1,0:T(8,128)(2,1)S(1)}, u32[]{:S(2)}, u32[]{:S(2)}) collective-permute-start(bf16[144,4096]{1,0:T(8,128)(2,1)S(1)} %slice.129), channel_id=1, source_target_pairs={{0,1},{1,0},{2,3},{3,2},{4,5},{5,4},{6,7},{7,6},{8,9},{9,8},{10,11... | collective-permute-start | bytes 3538952 | tf_op jit(solution)/shard_map/ppermute | solution.py:113
  228.6 15.2 %collective-permute-start.48 = (bf16[144,4096]{1,0:T(8,128)(2,1)S(1)}, bf16[144,4096]{1,0:T(8,128)(2,1)S(1)}, u32[]{:S(2)}, u32[]{:S(2)}) collective-permute-start(bf16[144,4096]{1,0:T(8,128)(2,1)S(1)} %slice.127), channel_id=1, source_target_pairs={{0,1},{1,0},{2,3},{3,2},{4,5},{5,4},{6,7},{7,6},{8,9},{9,8},{10,11... | collective-permute-start | bytes 3538952 | tf_op jit(solution)/shard_map/ppermute | solution.py:113
  244.2 15.2 %collective-permute-start.51 = (bf16[144,1024]{1,0:T(8,128)(2,1)S(1)}, bf16[144,1024]{1,0:T(8,128)(2,1)S(1)}, u32[]{:S(2)}, u32[]{:S(2)}) collective-permute-start(bf16[144,1024]{1,0:T(8,128)(2,1)S(1)} %get-tuple-element.151), channel_id=1, source_target_pairs={{0,24},{8,16},{16,8},{24,0},{1,25},{9,17},{17,9},{25,1},{2,26},{10... | collective-permute-start | bytes 884744 | tf_op jit(solution)/shard_map/ppermute | solution.py:238
  245.6 20.1 %collective-permute-start.50 = (bf16[144,1024]{1,0:T(8,128)(2,1)S(1)}, bf16[144,1024]{1,0:T(8,128)(2,1)S(1)}, u32[]{:S(2)}, u32[]{:S(2)}) collective-permute-start(bf16[144,1024]{1,0:T(8,128)(2,1)S(1)} %get-tuple-element.152), channel_id=1, source_target_pairs={{0,16},{8,24},{16,0},{24,8},{1,17},{9,25},{17,1},{25,9},{2,18},{10... | collective-permute-start | bytes 884744 | tf_op jit(solution)/shard_map/ppermute | solution.py:238
  246.8 20.1 %collective-permute-start.49 = (bf16[144,1024]{1,0:T(8,128)(2,1)S(1)}, bf16[144,1024]{1,0:T(8,128)(2,1)S(1)}, u32[]{:S(2)}, u32[]{:S(2)}) collective-permute-start(bf16[144,1024]{1,0:T(8,128)(2,1)S(1)} %get-tuple-element.153), channel_id=1, source_target_pairs={{0,8},{8,0},{16,24},{24,16},{1,9},{9,1},{17,25},{25,17},{2,10},{10... | collective-permute-start | bytes 884744 | tf_op jit(solution)/shard_map/ppermute | solution.py:238
  248.1 40.1 %collective-permute-start.55 = (bf16[144,1024]{1,0:T(8,128)(2,1)S(1)}, bf16[144,1024]{1,0:T(8,128)(2,1)S(1)}, u32[]{:S(2)}, u32[]{:S(2)}) collective-permute-start(bf16[144,1024]{1,0:T(8,128)(2,1)S(1)} %get-tuple-element.147), channel_id=1, source_target_pairs={{0,24},{8,16},{16,8},{24,0},{1,25},{9,17},{17,9},{25,1},{2,26},{10... | collective-permute-start | bytes 884744 | tf_op jit(solution)/shard_map/ppermute | solution.py:238
  253.1 35.2 %collective-permute-start.54 = (bf16[144,1024]{1,0:T(8,128)(2,1)S(1)}, bf16[144,1024]{1,0:T(8,128)(2,1)S(1)}, u32[]{:S(2)}, u32[]{:S(2)}) collective-permute-start(bf16[144,1024]{1,0:T(8,128)(2,1)S(1)} %get-tuple-element.148), channel_id=1, source_target_pairs={{0,16},{8,24},{16,0},{24,8},{1,17},{9,25},{17,1},{25,9},{2,18},{10... | collective-permute-start | bytes 884744 | tf_op jit(solution)/shard_map/ppermute | solution.py:238
  259.3 28.9 %collective-permute-start.53 = (bf16[144,1024]{1,0:T(8,128)(2,1)S(1)}, bf16[144,1024]{1,0:T(8,128)(2,1)S(1)}, u32[]{:S(2)}, u32[]{:S(2)}) collective-permute-start(bf16[144,1024]{1,0:T(8,128)(2,1)S(1)} %get-tuple-element.149), channel_id=1, source_target_pairs={{0,8},{8,0},{16,24},{24,16},{1,9},{9,1},{17,25},{25,17},{2,10},{10... | collective-permute-start | bytes 884744 | tf_op jit(solution)/shard_map/ppermute | solution.py:238
  265.7 17.9 %collective-permute-start.46 = (bf16[144,1024]{1,0:T(8,128)(2,1)S(1)}, bf16[144,1024]{1,0:T(8,128)(2,1)S(1)}, u32[]{:S(2)}, u32[]{:S(2)}) collective-permute-start(bf16[144,1024]{1,0:T(8,128)(2,1)S(1)} %get-tuple-element.156), channel_id=1, source_target_pairs={{0,16},{8,24},{16,0},{24,8},{1,17},{9,25},{17,1},{25,9},{2,18},{10... | collective-permute-start | bytes 884744 | tf_op jit(solution)/shard_map/ppermute | solution.py:238
  266.9 16.7 %collective-permute-start.45 = (bf16[144,1024]{1,0:T(8,128)(2,1)S(1)}, bf16[144,1024]{1,0:T(8,128)(2,1)S(1)}, u32[]{:S(2)}, u32[]{:S(2)}) collective-permute-start(bf16[144,1024]{1,0:T(8,128)(2,1)S(1)} %get-tuple-element.157), channel_id=1, source_target_pairs={{0,8},{8,0},{16,24},{24,16},{1,9},{9,1},{17,25},{25,17},{2,10},{10... | collective-permute-start | bytes 884744 | tf_op jit(solution)/shard_map/ppermute | solution.py:238
  (47 other events, 439.9 us)

commit v2 on v1

--- a/solution.py
+++ b/solution.py
@@ -15,7 +15,7 @@
 
 def adam_kernel(count, order_ref, *refs):
     pieces, (master, first, second) = refs[:count], refs[count:count + 3]
-    new_master, new_first, new_second = refs[count + 3:]
+    new_master, new_first, new_second = refs[-3:]
     turn = pl.program_id(0)
     grads = pieces[0][...].astype(jnp.float32)
     for other in range(1, count):
@@ -29,25 +29,34 @@
     new_second[0] = second_new
 
 
-def adam_update(order, pieces, master, first, second):
+def adam_update(order, pieces, master, first, second, calls=1):
     count, units, cols = master.shape
-    state = pl.BlockSpec((1, units, cols), lambda t, order: (order[t], 0, 0))
-    piece = pl.BlockSpec((units, cols), lambda t, order: (0, 0))
-    return pl.pallas_call(
-        functools.partial(adam_kernel, count),
-        grid_spec=pltpu.PrefetchScalarGridSpec(
-            num_scalar_prefetch=1,
-            grid=(count,),
-            in_specs=[piece] * count + [state] * 3,
-            out_specs=[state] * 3,
-        ),
-        out_shape=[jax.ShapeDtypeStruct(master.shape, jnp.float32)] * 3,
-        compiler_params=pltpu.CompilerParams(vmem_limit_bytes=20 << 20),
-        cost_estimate=pl.CostEstimate(
-            flops=16 * master.size, transcendentals=master.size, bytes_accessed=26 * master.size
-        ),
-        name="adam",
-    )(order, *pieces, master, first, second)
+    calls = calls if count % calls == 0 else 1
+    turns = count // calls
+    done = []
+    for call in range(calls):
+        low = call * turns
+        state = pl.BlockSpec((1, units, cols), lambda t, order, low=low: (order[t + low], 0, 0))
+        piece = pl.BlockSpec((units, cols), lambda t, order: (0, 0))
+        done = pl.pallas_call(
+            functools.partial(adam_kernel, turns),
+            grid_spec=pltpu.PrefetchScalarGridSpec(
+                num_scalar_prefetch=1,
+                grid=(turns,),
+                in_specs=[piece] * turns + [state] * 3 + [pl.BlockSpec(memory_space=pl.ANY)] * len(done),
+                out_specs=[state] * 3,
+            ),
+            out_shape=[jax.ShapeDtypeStruct(master.shape, jnp.float32)] * 3,
+            input_output_aliases={turns + 4 + i: i for i in range(len(done))},
+            compiler_params=pltpu.CompilerParams(vmem_limit_bytes=20 << 20),
+            cost_estimate=pl.CostEstimate(
+                flops=16 * master.size // calls,
+                transcendentals=master.size // calls,
+                bytes_accessed=26 * master.size // calls,
+            ),
+            name="adam",
+        )(order, *pieces[low:low + turns], master, first, second, *done)
+    return done
 
 
 def join_kernel(count, order_ref, *refs):
@@ -246,7 +255,8 @@
             ]
             pieces = trade(pieces)
             whole = join(order, pieces)
-            both = jnp.concatenate([whole, swap_cores(whole, chips)], axis=0)
+            partner_half = swap_cores(whole, chips)
+            both = jnp.concatenate([whole, partner_half], axis=0)
             return lax.optimization_barrier(both)
 
         gate_w, up_w, down_w = fetch(gate_master), fetch(up_master), fetch(down_master)
@@ -392,7 +402,7 @@
         up_grads = collect(d_up, tokens)
         down_new = adam_update(order, down_grads, down_master, down_first, down_second)
         gate_new = adam_update(order, gate_grads, gate_master, gate_first, gate_second)
-        up_new = adam_update(order, up_grads, up_master, up_first, up_second)
+        up_new = adam_update(order, up_grads, up_master, up_first, up_second, calls=4)
         return (
             out_rows, input_grads,
             gate_new[0], up_new[0], down_new[0],

time: 294 us -> 294 us (level)
  waiting for transfers between devices: 153 us -> 148 us
  Pallas kernels: 18.7 us -> 22.4 us
    ppermute x18, waiting for transfers between devices: 38.8 us -> 34.5 us  [trade(): lax.ppermute(pieces[turn], 'expert', [(e, partner(e, turn, experts)) for...]
    pallas_call x3 -> x6, Pallas kernels: 13.8 us -> 17.5 us  [adam_update(): pl.pallas_call(functools.partial(adam_kernel, turns), grid_spec=pltpu.Pre...]
  transfers between devices with their start and end apart: 56 -> 56, of which waited for: 27 -> 27; matrix products, arithmetic and copies ran while one was open for 18% -> 19% of each run, Pallas kernels for 5% -> 6%
where the time goes in v2:
time: 294 us
  waiting for transfers between devices  148 us (50%)
  starting transfers between devices  60.9 us (21%)
  matrix products  28.7 us (10%)
  Pallas kernels  22.4 us (8%)
  other arithmetic  20.6 us (7%)
  local copies, waits for them, and re-layouts  10.7 us (4%)
    ppermute x32, waiting for transfers between devices, hop(): return lax.ppermute(value, 'cuts', pairs)  114 us
    ppermute x18, waiting for transfers between devices, trade(): lax.ppermute(pieces[turn], 'expert', [(e, partner(e, turn, experts)) for...  34.5 us
    ppermute x32, starting transfers between devices, hop(): return lax.ppermute(value, 'cuts', pairs)  34.4 us
    ppermute x18, starting transfers between devices, trade(): lax.ppermute(pieces[turn], 'expert', [(e, partner(e, turn, experts)) for...  24.7 us
    pallas_call x6, Pallas kernels, adam_update(): pl.pallas_call(functools.partial(adam_kernel, turns), grid_spec=pltpu.Pre...  17.5 us
    dot_general x9, matrix products, dot_t(): lax.dot_general(a, b, (((1,), (1,)), ((), ())), preferred_element_type=jn...  12.6 us
    dot_general x9, matrix products, dot_n(): lax.dot_general(a, b, (((1,), (0,)), ((), ())), preferred_element_type=jn...  9.1 us
    select_n x20, other arithmetic, pick(): result = jnp.where(here, value, result)  7.05 us
  transfers between devices with their start and end apart: 56, of which 27 were waited for; matrix products, arithmetic and copies ran while one was open for 19% of the time, Pallas kernels for 6%

profile of v2, /device:TPU:0, one launch (start us, length us, event | category | flops | bytes accessed | tf_op | source)
XLA Modules:
  0.0 293.6 jit_solution(11452438976088480132)
XLA Ops:
  0.7 2.7 fusion.46
  3.4 3.9 %collective-permute-start.7 = (bf16[144,1024]{1,0:T(8,128)(2,1)}, bf16[144,1024]{1,0:T(8,128)(2,1)S(1)}, u32[]{:S(2)}, u32[]{:S(2)}) collective-permute-start(bf16[144,1024]{1,0:T(8,128)(2,1)} %get-tuple-element.157), channel_id=1, source_target_pairs={{0,24},{8,16},{16,8},{24,0},{1,25},{9,17},{17,9},{25,1},{2,26},{10... | collective-permute-start | bytes 884744 | tf_op jit(solution)/shard_map/ppermute | solution.py:247
  8.9 2.9 collective-permute-start.11
  15.5 2.1 collective-permute-start.1
  19.3 2.6 collective-permute-done.6.refs_2_
  25.9 2.3 collective-permute-done.11.refs_3_
  30.2 4.3 %collective-permute-done.10.refs_2_ = bf16[144,1024]{1,0:T(8,128)(2,1)} collective-permute-done((bf16[144,1024]{1,0:T(8,128)(2,1)}, bf16[144,1024]{1,0:T(8,128)(2,1)}, u32[]{:S(2)}, u32[]{:S(2)}) %collective-permute-start.10) | collective-permute-done | bytes 294944 | tf_op jit(solution)/shard_map/ppermute | solution.py:247
  39.7 2.0 join.4
  41.8 2.0 collective-permute-start.4
  43.8 2.4 collective-permute-done.14.refs_2_
  50.2 4.7 %collective-permute-done.4 = bf16[144,2048]{1,0:T(8,128)(2,1)S(1)} collective-permute-done((bf16[144,2048]{1,0:T(8,128)(2,1)S(1)}, bf16[144,2048]{1,0:T(8,128)(2,1)S(1)}, u32[]{:S(2)}, u32[]{:S(2)}) %collective-permute-start.4) | collective-permute-done | bytes 589856 | tf_op jit(solution)/shard_map/ppermute | solution.py:117
  54.9 2.5 collective-permute-start.17
  57.5 2.8 collective-permute-done.3
  62.0 2.8 collective-permute-done.17
  72.4 9.1 %collective-permute-done.2 = bf16[144,2048]{1,0:T(8,128)(2,1)S(1)} collective-permute-done((bf16[144,2048]{1,0:T(8,128)(2,1)S(1)}, bf16[144,2048]{1,0:T(8,128)(2,1)S(1)}, u32[]{:S(2)}, u32[]{:S(2)}) %collective-permute-start.2) | collective-permute-done | bytes 589856 | tf_op jit(solution)/shard_map/ppermute | solution.py:117
  81.7 2.0 collective-permute-start.23
  83.7 10.4 %collective-permute-done.18 = bf16[144,2048]{1,0:T(8,128)(2,1)S(1)} collective-permute-done((bf16[144,2048]{1,0:T(8,128)(2,1)S(1)}, bf16[144,2048]{1,0:T(8,128)(2,1)S(1)}, u32[]{:S(2)}, u32[]{:S(2)}) %collective-permute-start.18) | collective-permute-done | bytes 589856 | tf_op jit(solution)/shard_map/ppermute | solution.py:117
  99.1 2.0 collective-permute-start.21
  101.1 4.5 %collective-permute-done.24 = bf16[144,2048]{1,0:T(8,128)(2,1)S(1)} collective-permute-done((bf16[144,2048]{1,0:T(8,128)(2,1)S(1)}, bf16[144,2048]{1,0:T(8,128)(2,1)S(1)}, u32[]{:S(2)}, u32[]{:S(2)}) %collective-permute-start.24) | collective-permute-done | bytes 589856 | tf_op jit(solution)/shard_map/ppermute | solution.py:117
  106.0 2.0 collective-permute-start.28
  108.1 10.2 %collective-permute-done.22 = bf16[144,2048]{1,0:T(8,128)(2,1)S(1)} collective-permute-done((bf16[144,2048]{1,0:T(8,128)(2,1)S(1)}, bf16[144,2048]{1,0:T(8,128)(2,1)S(1)}, u32[]{:S(2)}, u32[]{:S(2)}) %collective-permute-start.22) | collective-permute-done | bytes 589856 | tf_op jit(solution)/shard_map/ppermute | solution.py:117
  123.2 2.0 collective-permute-start.29
  125.2 5.7 %collective-permute-done.25 = bf16[144,2048]{1,0:T(8,128)(2,1)S(1)} collective-permute-done((bf16[144,2048]{1,0:T(8,128)(2,1)S(1)}, bf16[144,2048]{1,0:T(8,128)(2,1)S(1)}, u32[]{:S(2)}, u32[]{:S(2)}) %collective-permute-start.25) | collective-permute-done | bytes 589856 | tf_op jit(solution)/shard_map/ppermute | solution.py:117
  131.3 2.0 collective-permute-start.31
  133.3 10.3 %collective-permute-done.27 = bf16[144,2048]{1,0:T(8,128)(2,1)S(1)} collective-permute-done((bf16[144,2048]{1,0:T(8,128)(2,1)S(1)}, bf16[144,2048]{1,0:T(8,128)(2,1)S(1)}, u32[]{:S(2)}, u32[]{:S(2)}) %collective-permute-start.27) | collective-permute-done | bytes 589856 | tf_op jit(solution)/shard_map/ppermute | solution.py:117
  149.1 7.1 %collective-permute-done.26 = bf16[144,2048]{1,0:T(8,128)(2,1)S(1)} collective-permute-done((bf16[144,2048]{1,0:T(8,128)(2,1)S(1)}, bf16[144,2048]{1,0:T(8,128)(2,1)S(1)}, u32[]{:S(2)}, u32[]{:S(2)}) %collective-permute-start.26) | collective-permute-done | bytes 589856 | tf_op jit(solution)/shard_map/ppermute | solution.py:117
  159.5 9.4 %collective-permute-done.30 = bf16[144,2048]{1,0:T(8,128)(2,1)S(1)} collective-permute-done((bf16[144,2048]{1,0:T(8,128)(2,1)S(1)}, bf16[144,2048]{1,0:T(8,128)(2,1)S(1)}, u32[]{:S(2)}, u32[]{:S(2)}) %collective-permute-start.30) | collective-permute-done | bytes 589856 | tf_op jit(solution)/shard_map/ppermute | solution.py:117
  177.8 3.7 %collective-permute-done.32 = bf16[144,2048]{1,0:T(8,128)(2,1)S(1)} collective-permute-done((bf16[144,2048]{1,0:T(8,128)(2,1)S(1)}, bf16[144,2048]{1,0:T(8,128)(2,1)S(1)}, u32[]{:S(2)}, u32[]{:S(2)}) %collective-permute-start.32) | collective-permute-done | bytes 589856 | tf_op jit(solution)/shard_map/ppermute | solution.py:117
  183.5 2.0 collective-permute-start.37
  185.5 8.7 %collective-permute-done.34 = bf16[144,2048]{1,0:T(8,128)(2,1)} collective-permute-done((bf16[144,2048]{1,0:T(8,128)(2,1)}, bf16[144,2048]{1,0:T(8,128)(2,1)}, u32[]{:S(2)}, u32[]{:S(2)}) %collective-permute-start.34) | collective-permute-done | bytes 589856 | tf_op jit(solution)/shard_map/ppermute | solution.py:117
  194.2 2.2 select_select_fusion
  200.6 2.3 convolution_convert_fusion
  202.9 2.3 convolution_convert_fusion.2
  205.2 2.5 convolution_convert_fusion.1
  212.3 2.0 collective-permute-start.43
  214.3 2.0 collective-permute-start.41
  219.3 9.1 %collective-permute-done.42 = bf16[144,2048]{1,0:T(8,128)(2,1)S(1)} collective-permute-done((bf16[144,2048]{1,0:T(8,128)(2,1)S(1)}, bf16[144,2048]{1,0:T(8,128)(2,1)S(1)}, u32[]{:S(2)}, u32[]{:S(2)}) %collective-permute-start.42) | collective-permute-done | bytes 589856 | tf_op jit(solution)/shard_map/ppermute | solution.py:117
  229.0 12.1 %collective-permute-done.40 = bf16[144,2048]{1,0:T(8,128)(2,1)S(1)} collective-permute-done((bf16[144,2048]{1,0:T(8,128)(2,1)S(1)}, bf16[144,2048]{1,0:T(8,128)(2,1)S(1)}, u32[]{:S(2)}, u32[]{:S(2)}) %collective-permute-start.40) | collective-permute-done | bytes 589856 | tf_op jit(solution)/shard_map/ppermute | solution.py:117
  249.5 3.4 %collective-permute-done.47.refs_3_ = bf16[144,1024]{1,0:T(8,128)(2,1)S(1)} collective-permute-done((bf16[144,1024]{1,0:T(8,128)(2,1)S(1)}, bf16[144,1024]{1,0:T(8,128)(2,1)S(1)}, u32[]{:S(2)}, u32[]{:S(2)}) %collective-permute-start.47) | collective-permute-done | bytes 294944 | tf_op jit(solution)/shard_map/ppermute | solution.py:247
  254.1 4.9 %collective-permute-done.51.refs_0_ = bf16[144,1024]{1,0:T(8,128)(2,1)S(1)} collective-permute-done((bf16[144,1024]{1,0:T(8,128)(2,1)S(1)}, bf16[144,1024]{1,0:T(8,128)(2,1)S(1)}, u32[]{:S(2)}, u32[]{:S(2)}) %collective-permute-start.51) | collective-permute-done | bytes 294944 | tf_op jit(solution)/shard_map/ppermute | solution.py:247
  260.4 5.2 %collective-permute-done.49.refs_0_ = bf16[144,1024]{1,0:T(8,128)(2,1)S(1)} collective-permute-done((bf16[144,1024]{1,0:T(8,128)(2,1)S(1)}, bf16[144,1024]{1,0:T(8,128)(2,1)S(1)}, u32[]{:S(2)}, u32[]{:S(2)}) %collective-permute-start.49) | collective-permute-done | bytes 294944 | tf_op jit(solution)/shard_map/ppermute | solution.py:247
  266.8 2.1 adam.7
  268.9 2.1 adam.8
  271.0 2.1 adam.9
  273.1 2.1 adam.10
  275.2 8.4 %collective-permute-done.46.refs_2_ = bf16[144,1024]{1,0:T(8,128)(2,1)S(1)} collective-permute-done((bf16[144,1024]{1,0:T(8,128)(2,1)S(1)}, bf16[144,1024]{1,0:T(8,128)(2,1)S(1)}, u32[]{:S(2)}, u32[]{:S(2)}) %collective-permute-start.46) | collective-permute-done | bytes 294944 | tf_op jit(solution)/shard_map/ppermute | solution.py:247
  283.6 4.6 %adam.6 = (f32[4,144,1024]{2,1,0:T(8,128)}, f32[4,144,1024]{2,1,0:T(8,128)}, f32[4,144,1024]{2,1,0:T(8,128)}) custom-call(s32[4]{0:T(128)S(1)} %pad_add_fusion.order_ref, bf16[144,1024]{1,0:T(8,128)(2,1)S(1)} %get-tuple-element.176.refs_0_, bf16[144,1024]{1,0:T(8,128)(2,1)S(1)} %collective-permute-done.45.refs_1_, ...), custom_call_target="tpu_custom_call" | custom-call | flops 9437184 | bytes 15335424 | tf_op jit(solution)/shard_map/adam/pallas_call | solution.py:41
  289.0 4.6 %adam.11 = (f32[4,144,1024]{2,1,0:T(8,128)}, f32[4,144,1024]{2,1,0:T(8,128)}, f32[4,144,1024]{2,1,0:T(8,128)}) custom-call(s32[4]{0:T(128)S(1)} %pad_add_fusion.order_ref, bf16[144,1024]{1,0:T(8,128)(2,1)S(1)} %get-tuple-element.168.refs_0_, bf16[144,1024]{1,0:T(8,128)(2,1)S(1)} %collective-permute-done.53.refs_1_, ...), custom_call_target="tpu_custom_call" | custom-call | flops 9437184 | bytes 15335424 | tf_op jit(solution)/shard_map/adam/pallas_call | solution.py:41
  (239 shorter events, 86.5 us)
Async XLA Ops:
  7.3 14.5 %collective-permute-start.6 = (bf16[144,1024]{1,0:T(8,128)(2,1)}, bf16[144,1024]{1,0:T(8,128)(2,1)S(1)}, u32[]{:S(2)}, u32[]{:S(2)}) collective-permute-start(bf16[144,1024]{1,0:T(8,128)(2,1)} %get-tuple-element.158), channel_id=1, source_target_pairs={{0,16},{8,24},{16,0},{24,8},{1,17},{9,25},{17,1},{25,9},{2,18},{10... | collective-permute-start | bytes 884744 | tf_op jit(solution)/shard_map/ppermute | solution.py:247
  7.9 16.5 %collective-permute-start.5 = (bf16[144,1024]{1,0:T(8,128)(2,1)}, bf16[144,1024]{1,0:T(8,128)(2,1)}, u32[]{:S(2)}, u32[]{:S(2)}) collective-permute-start(bf16[144,1024]{1,0:T(8,128)(2,1)} %get-tuple-element.159), channel_id=1, source_target_pairs={{0,8},{8,0},{16,24},{24,16},{1,9},{9,1},{17,25},{25,17},{2,10},{10... | collective-permute-start | bytes 884744 | tf_op jit(solution)/shard_map/ppermute | solution.py:247
  8.9 19.3 %collective-permute-start.11 = (bf16[144,1024]{1,0:T(8,128)(2,1)}, bf16[144,1024]{1,0:T(8,128)(2,1)}, u32[]{:S(2)}, u32[]{:S(2)}) collective-permute-start(bf16[144,1024]{1,0:T(8,128)(2,1)} %get-tuple-element.161), channel_id=1, source_target_pairs={{0,24},{8,16},{16,8},{24,0},{1,25},{9,17},{17,9},{25,1},{2,26},{10... | collective-permute-start | bytes 884744 | tf_op jit(solution)/shard_map/ppermute | solution.py:247
  11.8 22.8 %collective-permute-start.10 = (bf16[144,1024]{1,0:T(8,128)(2,1)}, bf16[144,1024]{1,0:T(8,128)(2,1)}, u32[]{:S(2)}, u32[]{:S(2)}) collective-permute-start(bf16[144,1024]{1,0:T(8,128)(2,1)} %get-tuple-element.162), channel_id=1, source_target_pairs={{0,16},{8,24},{16,0},{24,8},{1,17},{9,25},{17,1},{25,9},{2,18},{10... | collective-permute-start | bytes 884744 | tf_op jit(solution)/shard_map/ppermute | solution.py:247
  15.5 33.2 %collective-permute-start.1 = (bf16[144,2048]{1,0:T(8,128)(2,1)}, bf16[144,2048]{1,0:T(8,128)(2,1)S(1)}, u32[]{:S(2)}, u32[]{:S(2)}) collective-permute-start(bf16[144,2048]{1,0:T(8,128)(2,1)} %get-tuple-element.181), channel_id=1, source_target_pairs={{0,2},{2,4},{4,6},{6,7},{7,5},{5,3},{3,1},{1,0},{8,10},{10,12},{12... | collective-permute-start | bytes 1769480 | tf_op jit(solution)/shard_map/ppermute | solution.py:117
  21.8 15.8 %collective-permute-start.9 = (bf16[144,1024]{1,0:T(8,128)(2,1)S(1)}, bf16[144,1024]{1,0:T(8,128)(2,1)S(1)}, u32[]{:S(2)}, u32[]{:S(2)}) collective-permute-start(bf16[144,1024]{1,0:T(8,128)(2,1)S(1)} %copy-done.24), channel_id=1, source_target_pairs={{0,8},{8,0},{16,24},{24,16},{1,9},{9,1},{17,25},{25,17},{2,10},{10... | collective-permute-start | bytes 884744 | tf_op jit(solution)/shard_map/ppermute | solution.py:247
  24.4 17.4 %collective-permute-start.15 = (bf16[144,1024]{1,0:T(8,128)(2,1)S(1)}, bf16[144,1024]{1,0:T(8,128)(2,1)S(1)}, u32[]{:S(2)}, u32[]{:S(2)}) collective-permute-start(bf16[144,1024]{1,0:T(8,128)(2,1)S(1)} %get-tuple-element.153), channel_id=1, source_target_pairs={{0,24},{8,16},{16,8},{24,0},{1,25},{9,17},{17,9},{25,1},{2,26},{10... | collective-permute-start | bytes 884744 | tf_op jit(solution)/shard_map/ppermute | solution.py:247
  28.2 17.9 %collective-permute-start.14 = (bf16[144,1024]{1,0:T(8,128)(2,1)S(1)}, bf16[144,1024]{1,0:T(8,128)(2,1)S(1)}, u32[]{:S(2)}, u32[]{:S(2)}) collective-permute-start(bf16[144,1024]{1,0:T(8,128)(2,1)S(1)} %get-tuple-element.154), channel_id=1, source_target_pairs={{0,16},{8,24},{16,0},{24,8},{1,17},{9,25},{17,1},{25,9},{2,18},{10... | collective-permute-start | bytes 884744 | tf_op jit(solution)/shard_map/ppermute | solution.py:247
  46.5 20.1 %collective-permute-start.12 = (bf16[144,4096]{1,0:T(8,128)(2,1)S(1)}, bf16[144,4096]{1,0:T(8,128)(2,1)S(1)}, u32[]{:S(2)}, u32[]{:S(2)}) collective-permute-start(bf16[144,4096]{1,0:T(8,128)(2,1)S(1)} %join.4), channel_id=1, source_target_pairs={{0,1},{1,0},{2,3},{3,2},{4,5},{5,4},{6,7},{7,6},{8,9},{9,8},{10,11... | collective-permute-start | bytes 3538952 | tf_op jit(solution)/shard_map/ppermute | solution.py:122
  48.7 19.7 %collective-permute-start.16 = (bf16[144,4096]{1,0:T(8,128)(2,1)S(1)}, bf16[144,4096]{1,0:T(8,128)(2,1)S(1)}, u32[]{:S(2)}, u32[]{:S(2)}) collective-permute-start(bf16[144,4096]{1,0:T(8,128)(2,1)S(1)} %join.5), channel_id=1, source_target_pairs={{0,1},{1,0},{2,3},{3,2},{4,5},{5,4},{6,7},{7,6},{8,9},{9,8},{10,11... | collective-permute-start | bytes 3538952 | tf_op jit(solution)/shard_map/ppermute | solution.py:122
  50.1 18.6 %collective-permute-start.8 = (bf16[144,4096]{1,0:T(8,128)(2,1)S(1)}, bf16[144,4096]{1,0:T(8,128)(2,1)S(1)}, u32[]{:S(2)}, u32[]{:S(2)}) collective-permute-start(bf16[144,4096]{1,0:T(8,128)(2,1)S(1)} %join.3), channel_id=1, source_target_pairs={{0,1},{1,0},{2,3},{3,2},{4,5},{5,4},{6,7},{7,6},{8,9},{9,8},{10,11... | collective-permute-start | bytes 3538952 | tf_op jit(solution)/shard_map/ppermute | solution.py:122
  60.2 21.4 %collective-permute-start.19 = (bf16[144,2048]{1,0:T(8,128)(2,1)S(1)}, bf16[144,2048]{1,0:T(8,128)(2,1)S(1)}, u32[]{:S(2)}, u32[]{:S(2)}) collective-permute-start(bf16[144,2048]{1,0:T(8,128)(2,1)S(1)} %broadcast_select_fusion.2), channel_id=1, source_target_pairs={{0,2},{2,4},{4,6},{6,7},{7,5},{5,3},{3,1},{1,0},{8,10},{10,12},{12... | collective-permute-start | bytes 1769480 | tf_op jit(solution)/shard_map/ppermute | solution.py:117
  64.8 16.7 %collective-permute-start.2 = (bf16[144,2048]{1,0:T(8,128)(2,1)S(1)}, bf16[144,2048]{1,0:T(8,128)(2,1)S(1)}, u32[]{:S(2)}, u32[]{:S(2)}) collective-permute-start(bf16[144,2048]{1,0:T(8,128)(2,1)S(1)} %get-tuple-element.210), channel_id=1, source_target_pairs={{2,0},{4,2},{6,4},{7,6},{5,7},{3,5},{1,3},{0,1},{10,8},{12,10},{14... | collective-permute-start | bytes 1769480 | tf_op jit(solution)/shard_map/ppermute | solution.py:117
  66.6 27.5 %collective-permute-start.18 = (bf16[144,2048]{1,0:T(8,128)(2,1)S(1)}, bf16[144,2048]{1,0:T(8,128)(2,1)S(1)}, u32[]{:S(2)}, u32[]{:S(2)}) collective-permute-start(bf16[144,2048]{1,0:T(8,128)(2,1)S(1)} %get-tuple-element.212), channel_id=1, source_target_pairs={{2,0},{4,2},{6,4},{7,6},{5,7},{3,5},{1,3},{0,1},{10,8},{12,10},{14... | collective-permute-start | bytes 1769480 | tf_op jit(solution)/shard_map/ppermute | solution.py:117
  72.0 27.0 %collective-permute-start.20 = (bf16[144,2048]{1,0:T(8,128)(2,1)S(1)}, bf16[144,2048]{1,0:T(8,128)(2,1)S(1)}, u32[]{:S(2)}, u32[]{:S(2)}) collective-permute-start(bf16[144,2048]{1,0:T(8,128)(2,1)S(1)} %broadcast_select_fusion.1), channel_id=1, source_target_pairs={{0,2},{2,4},{4,6},{6,7},{7,5},{5,3},{3,1},{1,0},{8,10},{10,12},{12... | collective-permute-start | bytes 1769480 | tf_op jit(solution)/shard_map/ppermute | solution.py:117
  81.6 24.1 %collective-permute-start.24 = (bf16[144,2048]{1,0:T(8,128)(2,1)S(1)}, bf16[144,2048]{1,0:T(8,128)(2,1)S(1)}, u32[]{:S(2)}, u32[]{:S(2)}) collective-permute-start(bf16[144,2048]{1,0:T(8,128)(2,1)S(1)} %get-tuple-element.208), channel_id=1, source_target_pairs={{2,0},{4,2},{6,4},{7,6},{5,7},{3,5},{1,3},{0,1},{10,8},{12,10},{14... | collective-permute-start | bytes 1769480 | tf_op jit(solution)/shard_map/ppermute | solution.py:117
  81.7 24.2 %collective-permute-start.23 = (bf16[144,2048]{1,0:T(8,128)(2,1)S(1)}, bf16[144,2048]{1,0:T(8,128)(2,1)S(1)}, u32[]{:S(2)}, u32[]{:S(2)}) collective-permute-start(bf16[144,2048]{1,0:T(8,128)(2,1)S(1)} %broadcast_select_fusion), channel_id=1, source_target_pairs={{0,2},{2,4},{4,6},{6,7},{7,5},{5,3},{3,1},{1,0},{8,10},{10,12},{12... | collective-permute-start | bytes 1769480 | tf_op jit(solution)/shard_map/ppermute | solution.py:117
  95.8 22.5 %collective-permute-start.22 = (bf16[144,2048]{1,0:T(8,128)(2,1)S(1)}, bf16[144,2048]{1,0:T(8,128)(2,1)S(1)}, u32[]{:S(2)}, u32[]{:S(2)}) collective-permute-start(bf16[144,2048]{1,0:T(8,128)(2,1)S(1)} %get-tuple-element.205), channel_id=1, source_target_pairs={{2,0},{4,2},{6,4},{7,6},{5,7},{3,5},{1,3},{0,1},{10,8},{12,10},{14... | collective-permute-start | bytes 1769480 | tf_op jit(solution)/shard_map/ppermute | solution.py:117
  99.1 24.0 %collective-permute-start.21 = (bf16[144,2048]{1,0:T(8,128)(2,1)S(1)}, bf16[144,2048]{1,0:T(8,128)(2,1)S(1)}, u32[]{:S(2)}, u32[]{:S(2)}) collective-permute-start(bf16[144,2048]{1,0:T(8,128)(2,1)S(1)} %select_select_fusion.11), channel_id=1, source_target_pairs={{0,2},{2,4},{4,6},{6,7},{7,5},{5,3},{3,1},{1,0},{8,10},{10,12},{12... | collective-permute-start | bytes 1769480 | tf_op jit(solution)/shard_map/ppermute | solution.py:117
  105.9 25.0 %collective-permute-start.25 = (bf16[144,2048]{1,0:T(8,128)(2,1)S(1)}, bf16[144,2048]{1,0:T(8,128)(2,1)S(1)}, u32[]{:S(2)}, u32[]{:S(2)}) collective-permute-start(bf16[144,2048]{1,0:T(8,128)(2,1)S(1)} %get-tuple-element.202), channel_id=1, source_target_pairs={{2,0},{4,2},{6,4},{7,6},{5,7},{3,5},{1,3},{0,1},{10,8},{12,10},{14... | collective-permute-start | bytes 1769480 | tf_op jit(solution)/shard_map/ppermute | solution.py:117
  106.0 25.1 %collective-permute-start.28 = (bf16[144,2048]{1,0:T(8,128)(2,1)S(1)}, bf16[144,2048]{1,0:T(8,128)(2,1)S(1)}, u32[]{:S(2)}, u32[]{:S(2)}) collective-permute-start(bf16[144,2048]{1,0:T(8,128)(2,1)S(1)} %select_select_fusion.9), channel_id=1, source_target_pairs={{0,2},{2,4},{4,6},{6,7},{7,5},{5,3},{3,1},{1,0},{8,10},{10,12},{12... | collective-permute-start | bytes 1769480 | tf_op jit(solution)/shard_map/ppermute | solution.py:117
  123.1 20.5 %collective-permute-start.27 = (bf16[144,2048]{1,0:T(8,128)(2,1)S(1)}, bf16[144,2048]{1,0:T(8,128)(2,1)S(1)}, u32[]{:S(2)}, u32[]{:S(2)}) collective-permute-start(bf16[144,2048]{1,0:T(8,128)(2,1)S(1)} %get-tuple-element.204), channel_id=1, source_target_pairs={{2,0},{4,2},{6,4},{7,6},{5,7},{3,5},{1,3},{0,1},{10,8},{12,10},{14... | collective-permute-start | bytes 1769480 | tf_op jit(solution)/shard_map/ppermute | solution.py:117
  123.2 23.7 %collective-permute-start.29 = (bf16[144,2048]{1,0:T(8,128)(2,1)S(1)}, bf16[144,2048]{1,0:T(8,128)(2,1)S(1)}, u32[]{:S(2)}, u32[]{:S(2)}) collective-permute-start(bf16[144,2048]{1,0:T(8,128)(2,1)S(1)} %select_add_fusion.15), channel_id=1, source_target_pairs={{0,2},{2,4},{4,6},{6,7},{7,5},{5,3},{3,1},{1,0},{8,10},{10,12},{12... | collective-permute-start | bytes 1769480 | tf_op jit(solution)/shard_map/ppermute | solution.py:117
  131.1 25.1 %collective-permute-start.26 = (bf16[144,2048]{1,0:T(8,128)(2,1)S(1)}, bf16[144,2048]{1,0:T(8,128)(2,1)S(1)}, u32[]{:S(2)}, u32[]{:S(2)}) collective-permute-start(bf16[144,2048]{1,0:T(8,128)(2,1)S(1)} %get-tuple-element.198), channel_id=1, source_target_pairs={{2,0},{4,2},{6,4},{7,6},{5,7},{3,5},{1,3},{0,1},{10,8},{12,10},{14... | collective-permute-start | bytes 1769480 | tf_op jit(solution)/shard_map/ppermute | solution.py:117
  131.3 25.2 %collective-permute-start.31 = (bf16[144,2048]{1,0:T(8,128)(2,1)S(1)}, bf16[144,2048]{1,0:T(8,128)(2,1)S(1)}, u32[]{:S(2)}, u32[]{:S(2)}) collective-permute-start(bf16[144,2048]{1,0:T(8,128)(2,1)S(1)} %select_add_fusion.13), channel_id=1, source_target_pairs={{0,2},{2,4},{4,6},{6,7},{7,5},{5,3},{3,1},{1,0},{8,10},{10,12},{12... | collective-permute-start | bytes 1769480 | tf_op jit(solution)/shard_map/ppermute | solution.py:117
  143.9 25.0 %collective-permute-start.30 = (bf16[144,2048]{1,0:T(8,128)(2,1)S(1)}, bf16[144,2048]{1,0:T(8,128)(2,1)S(1)}, u32[]{:S(2)}, u32[]{:S(2)}) collective-permute-start(bf16[144,2048]{1,0:T(8,128)(2,1)S(1)} %get-tuple-element.200), channel_id=1, source_target_pairs={{2,0},{4,2},{6,4},{7,6},{5,7},{3,5},{1,3},{0,1},{10,8},{12,10},{14... | collective-permute-start | bytes 1769480 | tf_op jit(solution)/shard_map/ppermute | solution.py:117
  147.1 27.8 %collective-permute-start.33 = (bf16[144,2048]{1,0:T(8,128)(2,1)S(1)}, bf16[144,2048]{1,0:T(8,128)(2,1)S(1)}, u32[]{:S(2)}, u32[]{:S(2)}) collective-permute-start(bf16[144,2048]{1,0:T(8,128)(2,1)S(1)} %select_add_fusion.11), channel_id=1, source_target_pairs={{0,2},{2,4},{4,6},{6,7},{7,5},{5,3},{3,1},{1,0},{8,10},{10,12},{12... | collective-permute-start | bytes 1769480 | tf_op jit(solution)/shard_map/ppermute | solution.py:117
  156.5 25.0 %collective-permute-start.32 = (bf16[144,2048]{1,0:T(8,128)(2,1)S(1)}, bf16[144,2048]{1,0:T(8,128)(2,1)S(1)}, u32[]{:S(2)}, u32[]{:S(2)}) collective-permute-start(bf16[144,2048]{1,0:T(8,128)(2,1)S(1)} %get-tuple-element.194), channel_id=1, source_target_pairs={{2,0},{4,2},{6,4},{7,6},{5,7},{3,5},{1,3},{0,1},{10,8},{12,10},{14... | collective-permute-start | bytes 1769480 | tf_op jit(solution)/shard_map/ppermute | solution.py:117
  157.5 25.1 %collective-permute-start.35 = (bf16[144,2048]{1,0:T(8,128)(2,1)}, bf16[144,2048]{1,0:T(8,128)(2,1)S(1)}, u32[]{:S(2)}, u32[]{:S(2)}) collective-permute-start(bf16[144,2048]{1,0:T(8,128)(2,1)} %select_add_fusion.9), channel_id=1, source_target_pairs={{0,2},{2,4},{4,6},{6,7},{7,5},{5,3},{3,1},{1,0},{8,10},{10,12},{12... | collective-permute-start | bytes 1769480 | tf_op jit(solution)/shard_map/ppermute | solution.py:117
  170.0 24.2 %collective-permute-start.34 = (bf16[144,2048]{1,0:T(8,128)(2,1)}, bf16[144,2048]{1,0:T(8,128)(2,1)}, u32[]{:S(2)}, u32[]{:S(2)}) collective-permute-start(bf16[144,2048]{1,0:T(8,128)(2,1)} %get-tuple-element.196), channel_id=1, source_target_pairs={{2,0},{4,2},{6,4},{7,6},{5,7},{3,5},{1,3},{0,1},{10,8},{12,10},{14... | collective-permute-start | bytes 1769480 | tf_op jit(solution)/shard_map/ppermute | solution.py:117
  175.8 34.0 %collective-permute-start.39 = (bf16[144,2048]{1,0:T(8,128)(2,1)}, bf16[144,2048]{1,0:T(8,128)(2,1)S(1)}, u32[]{:S(2)}, u32[]{:S(2)}) collective-permute-start(bf16[144,2048]{1,0:T(8,128)(2,1)} %select_add_fusion.7), channel_id=1, source_target_pairs={{0,2},{2,4},{4,6},{6,7},{7,5},{5,3},{3,1},{1,0},{8,10},{10,12},{12... | collective-permute-start | bytes 1769480 | tf_op jit(solution)/shard_map/ppermute | solution.py:117
  182.5 27.4 %collective-permute-start.38 = (bf16[144,2048]{1,0:T(8,128)(2,1)}, bf16[144,2048]{1,0:T(8,128)(2,1)S(1)}, u32[]{:S(2)}, u32[]{:S(2)}) collective-permute-start(bf16[144,2048]{1,0:T(8,128)(2,1)} %get-tuple-element.190), channel_id=1, source_target_pairs={{2,0},{4,2},{6,4},{7,6},{5,7},{3,5},{1,3},{0,1},{10,8},{12,10},{14... | collective-permute-start | bytes 1769480 | tf_op jit(solution)/shard_map/ppermute | solution.py:117
  183.5 26.5 %collective-permute-start.37 = (bf16[144,2048]{1,0:T(8,128)(2,1)}, bf16[144,2048]{1,0:T(8,128)(2,1)S(1)}, u32[]{:S(2)}, u32[]{:S(2)}) collective-permute-start(bf16[144,2048]{1,0:T(8,128)(2,1)} %select_add_fusion.5), channel_id=1, source_target_pairs={{0,2},{2,4},{4,6},{6,7},{7,5},{5,3},{3,1},{1,0},{8,10},{10,12},{12... | collective-permute-start | bytes 1769480 | tf_op jit(solution)/shard_map/ppermute | solution.py:117
  209.7 31.9 %collective-permute-start.44 = (bf16[144,4096]{1,0:T(8,128)(2,1)S(1)}, bf16[144,4096]{1,0:T(8,128)(2,1)S(1)}, u32[]{:S(2)}, u32[]{:S(2)}) collective-permute-start(bf16[144,4096]{1,0:T(8,128)(2,1)S(1)} %slice.125), channel_id=1, source_target_pairs={{0,1},{1,0},{2,3},{3,2},{4,5},{5,4},{6,7},{7,6},{8,9},{9,8},{10,11... | collective-permute-start | bytes 3538952 | tf_op jit(solution)/shard_map/ppermute | solution.py:122
  212.2 16.2 %collective-permute-start.42 = (bf16[144,2048]{1,0:T(8,128)(2,1)S(1)}, bf16[144,2048]{1,0:T(8,128)(2,1)S(1)}, u32[]{:S(2)}, u32[]{:S(2)}) collective-permute-start(bf16[144,2048]{1,0:T(8,128)(2,1)S(1)} %select_add_fusion), channel_id=1, source_target_pairs={{2,0},{4,2},{6,4},{7,6},{5,7},{3,5},{1,3},{0,1},{10,8},{12,10},{14... | collective-permute-start | bytes 1769480 | tf_op jit(solution)/shard_map/ppermute | solution.py:117
  212.3 16.2 %collective-permute-start.43 = (bf16[144,2048]{1,0:T(8,128)(2,1)S(1)}, bf16[144,2048]{1,0:T(8,128)(2,1)S(1)}, u32[]{:S(2)}, u32[]{:S(2)}) collective-permute-start(bf16[144,2048]{1,0:T(8,128)(2,1)S(1)} %select_add_fusion.1), channel_id=1, source_target_pairs={{0,2},{2,4},{4,6},{6,7},{7,5},{5,3},{3,1},{1,0},{8,10},{10,12},{12... | collective-permute-start | bytes 1769480 | tf_op jit(solution)/shard_map/ppermute | solution.py:117
  214.3 26.7 %collective-permute-start.40 = (bf16[144,2048]{1,0:T(8,128)(2,1)S(1)}, bf16[144,2048]{1,0:T(8,128)(2,1)S(1)}, u32[]{:S(2)}, u32[]{:S(2)}) collective-permute-start(bf16[144,2048]{1,0:T(8,128)(2,1)S(1)} %select_add_fusion.2), channel_id=1, source_target_pairs={{2,0},{4,2},{6,4},{7,6},{5,7},{3,5},{1,3},{0,1},{10,8},{12,10},{14... | collective-permute-start | bytes 1769480 | tf_op jit(solution)/shard_map/ppermute | solution.py:117
  214.3 26.7 %collective-permute-start.41 = (bf16[144,2048]{1,0:T(8,128)(2,1)S(1)}, bf16[144,2048]{1,0:T(8,128)(2,1)S(1)}, u32[]{:S(2)}, u32[]{:S(2)}) collective-permute-start(bf16[144,2048]{1,0:T(8,128)(2,1)S(1)} %select_add_fusion.3), channel_id=1, source_target_pairs={{0,2},{2,4},{4,6},{6,7},{7,5},{5,3},{3,1},{1,0},{8,10},{10,12},{12... | collective-permute-start | bytes 1769480 | tf_op jit(solution)/shard_map/ppermute | solution.py:117
  228.4 19.0 %collective-permute-start.52 = (bf16[144,4096]{1,0:T(8,128)(2,1)S(1)}, bf16[144,4096]{1,0:T(8,128)(2,1)S(1)}, u32[]{:S(2)}, u32[]{:S(2)}) collective-permute-start(bf16[144,4096]{1,0:T(8,128)(2,1)S(1)} %slice.129), channel_id=1, source_target_pairs={{0,1},{1,0},{2,3},{3,2},{4,5},{5,4},{6,7},{7,6},{8,9},{9,8},{10,11... | collective-permute-start | bytes 3538952 | tf_op jit(solution)/shard_map/ppermute | solution.py:122
  228.5 15.1 %collective-permute-start.48 = (bf16[144,4096]{1,0:T(8,128)(2,1)S(1)}, bf16[144,4096]{1,0:T(8,128)(2,1)S(1)}, u32[]{:S(2)}, u32[]{:S(2)}) collective-permute-start(bf16[144,4096]{1,0:T(8,128)(2,1)S(1)} %slice.127), channel_id=1, source_target_pairs={{0,1},{1,0},{2,3},{3,2},{4,5},{5,4},{6,7},{7,6},{8,9},{9,8},{10,11... | collective-permute-start | bytes 3538952 | tf_op jit(solution)/shard_map/ppermute | solution.py:122
  243.9 15.0 %collective-permute-start.51 = (bf16[144,1024]{1,0:T(8,128)(2,1)S(1)}, bf16[144,1024]{1,0:T(8,128)(2,1)S(1)}, u32[]{:S(2)}, u32[]{:S(2)}) collective-permute-start(bf16[144,1024]{1,0:T(8,128)(2,1)S(1)} %get-tuple-element.170), channel_id=1, source_target_pairs={{0,8},{8,0},{16,24},{24,16},{1,9},{9,1},{17,25},{25,17},{2,10},{10... | collective-permute-start | bytes 884744 | tf_op jit(solution)/shard_map/ppermute | solution.py:247
  245.2 14.6 %collective-permute-start.50 = (bf16[144,1024]{1,0:T(8,128)(2,1)S(1)}, bf16[144,1024]{1,0:T(8,128)(2,1)S(1)}, u32[]{:S(2)}, u32[]{:S(2)}) collective-permute-start(bf16[144,1024]{1,0:T(8,128)(2,1)S(1)} %get-tuple-element.171), channel_id=1, source_target_pairs={{0,16},{8,24},{16,0},{24,8},{1,17},{9,25},{17,1},{25,9},{2,18},{10... | collective-permute-start | bytes 884744 | tf_op jit(solution)/shard_map/ppermute | solution.py:247
  246.1 19.6 %collective-permute-start.49 = (bf16[144,1024]{1,0:T(8,128)(2,1)S(1)}, bf16[144,1024]{1,0:T(8,128)(2,1)S(1)}, u32[]{:S(2)}, u32[]{:S(2)}) collective-permute-start(bf16[144,1024]{1,0:T(8,128)(2,1)S(1)} %get-tuple-element.172), channel_id=1, source_target_pairs={{0,24},{8,16},{16,8},{24,0},{1,25},{9,17},{17,9},{25,1},{2,26},{10... | collective-permute-start | bytes 884744 | tf_op jit(solution)/shard_map/ppermute | solution.py:247
  247.9 40.3 %collective-permute-start.55 = (bf16[144,1024]{1,0:T(8,128)(2,1)S(1)}, bf16[144,1024]{1,0:T(8,128)(2,1)S(1)}, u32[]{:S(2)}, u32[]{:S(2)}) collective-permute-start(bf16[144,1024]{1,0:T(8,128)(2,1)S(1)} %get-tuple-element.165), channel_id=1, source_target_pairs={{0,24},{8,16},{16,8},{24,0},{1,25},{9,17},{17,9},{25,1},{2,26},{10... | collective-permute-start | bytes 884744 | tf_op jit(solution)/shard_map/ppermute | solution.py:247
  252.9 35.3 %collective-permute-start.54 = (bf16[144,1024]{1,0:T(8,128)(2,1)S(1)}, bf16[144,1024]{1,0:T(8,128)(2,1)S(1)}, u32[]{:S(2)}, u32[]{:S(2)}) collective-permute-start(bf16[144,1024]{1,0:T(8,128)(2,1)S(1)} %get-tuple-element.166), channel_id=1, source_target_pairs={{0,16},{8,24},{16,0},{24,8},{1,17},{9,25},{17,1},{25,9},{2,18},{10... | collective-permute-start | bytes 884744 | tf_op jit(solution)/shard_map/ppermute | solution.py:247
  258.9 29.3 %collective-permute-start.53 = (bf16[144,1024]{1,0:T(8,128)(2,1)S(1)}, bf16[144,1024]{1,0:T(8,128)(2,1)S(1)}, u32[]{:S(2)}, u32[]{:S(2)}) collective-permute-start(bf16[144,1024]{1,0:T(8,128)(2,1)S(1)} %get-tuple-element.167), channel_id=1, source_target_pairs={{0,8},{8,0},{16,24},{24,16},{1,9},{9,1},{17,25},{25,17},{2,10},{10... | collective-permute-start | bytes 884744 | tf_op jit(solution)/shard_map/ppermute | solution.py:247
  259.8 23.8 %collective-permute-start.46 = (bf16[144,1024]{1,0:T(8,128)(2,1)S(1)}, bf16[144,1024]{1,0:T(8,128)(2,1)S(1)}, u32[]{:S(2)}, u32[]{:S(2)}) collective-permute-start(bf16[144,1024]{1,0:T(8,128)(2,1)S(1)} %get-tuple-element.174), channel_id=1, source_target_pairs={{0,16},{8,24},{16,0},{24,8},{1,17},{9,25},{17,1},{25,9},{2,18},{10... | collective-permute-start | bytes 884744 | tf_op jit(solution)/shard_map/ppermute | solution.py:247
  265.7 17.9 %collective-permute-start.45 = (bf16[144,1024]{1,0:T(8,128)(2,1)S(1)}, bf16[144,1024]{1,0:T(8,128)(2,1)S(1)}, u32[]{:S(2)}, u32[]{:S(2)}) collective-permute-start(bf16[144,1024]{1,0:T(8,128)(2,1)S(1)} %get-tuple-element.175), channel_id=1, source_target_pairs={{0,8},{8,0},{16,24},{24,16},{1,9},{9,1},{17,25},{25,17},{2,10},{10... | collective-permute-start | bytes 884744 | tf_op jit(solution)/shard_map/ppermute | solution.py:247
  (46 other events, 413.8 us)
